TPU v7x, 32 devices: a whole 2x2x4 slice. The times are simulated.
32 devices in a mesh: section: 2 (over core), ctx: 4 (over z), tp: 4 (over y, x).
Axes of the slice: x: 2, y: 2, z: 4, core: 2. Of those that a mesh axis runs over, the one named last changes fastest.
Arguments:
- q_raw: bfloat16 [2048, 3072], P(('section', 'ctx'), 'tp'), may hold values from -8000 to 8000
- k_raw: bfloat16 [2048, 3072], P(('section', 'ctx'), 'tp'), may hold values from -8000 to 8000
- values: bfloat16 [2048, 3072], P(('section', 'ctx'), 'tp'), may hold values from -6 to 6
- text_k: bfloat16 [512, 3072], P(('section', 'ctx'), 'tp'), may hold values from -8000 to 8000
- text_v: bfloat16 [512, 3072], P(('section', 'ctx'), 'tp'), may hold values from -6 to 6
- q_gain: float32 [3072], P('tp'), may hold values from 0.4 to 1.6
- k_gain: float32 [3072], P('tp'), may hold values from 0.4 to 1.6
- cotangent: bfloat16 [2048, 3072], P(('section', 'ctx'), 'tp'), may hold values from -80 to 80
- vid_len: int32 [1], replicated, may hold values from 1024 to 2048
- txt_len: int32 [1], replicated, may hold values from 384 to 512
Outputs:
- attention_out: bfloat16 [2048, 3072], P(('section', 'ctx'), 'tp')
- d_q_raw: bfloat16 [2048, 3072], P(('section', 'ctx'), 'tp')
- d_k_raw: bfloat16 [2048, 3072], P(('section', 'ctx'), 'tp')
- d_values: bfloat16 [2048, 3072], P(('section', 'ctx'), 'tp')
- d_text_k: bfloat16 [512, 3072], P(('section', 'ctx'), 'tp')
- d_text_v: bfloat16 [512, 3072], P(('section', 'ctx'), 'tp')
- d_q_gain: float32 [3072], P('tp')
- d_k_gain: float32 [3072], P('tp')
All inputs are finite; a program needn't handle non-finite values.
Results may differ from a plain program's by a relative error of at most 0.03.
Values may be sent and summed in bfloat16 or wider, within the bound.
No kernel may reach another device: no remote copies, remote signals or barrier semaphores. Data moves between devices by JAX's collectives and lax.ppermute only.
A program may use at most 64 MiB of HBM per device.

v0:
```python
import functools

import jax
import jax.numpy as jnp
import numpy as np
from jax import lax
from jax.experimental import pallas as pl
from jax.experimental.pallas import tpu as pltpu
from jax.sharding import PartitionSpec as P


HD = 128
EPS = 1e-06
NEG = -1e30
LOG2E = 1.4426950408889634
GROUP = ("section", "ctx")
BF = jnp.bfloat16
F32 = jnp.float32


VM = pl.BlockSpec(memory_space=pltpu.VMEM)
SM = pl.BlockSpec(memory_space=pltpu.SMEM)


def head_owners(members, chips, heads):
    order = sorted(range(members), key=lambda d: (abs(2 * (d % chips) - (chips - 1)), d))
    table = np.full((members,), -1, np.int32)
    for head, device in enumerate(order[:heads]):
        table[device] = head
    return table


def columns(head):
    return pl.ds(pl.multiple_of(head * HD, HD), HD)


def tile(i):
    return slice(i * HD, (i + 1) * HD)


def row_to_columns(row):
    return jnp.broadcast_to(row, (HD, row.shape[1])).T


def rows_to_row(block):
    return jnp.sum(block.T, axis=0, keepdims=True)


def nt(a, b):
    return lax.dot_general(a, b, (((1,), (1,)), ((), ())), preferred_element_type=F32)


def nn(a, b):
    return jnp.dot(a, b, preferred_element_type=F32)


def call(kernel, outs, ins, smem=0, scratch=(), flops=0, aliases=None, vmem=24, space=None):
    nbytes = sum(int(np.prod(o.shape)) * o.dtype.itemsize for o in list(outs) + list(ins)[smem:])
    big = VM if space is None else space
    return pl.pallas_call(
        kernel,
        out_shape=tuple(jax.ShapeDtypeStruct(o.shape, o.dtype) for o in outs),
        in_specs=[SM] * smem + [big] * (len(ins) - smem),
        out_specs=tuple(VM for _ in outs),
        scratch_shapes=list(scratch),
        input_output_aliases=aliases or {},
        compiler_params=pltpu.CompilerParams(vmem_limit_bytes=vmem << 20),
        cost_estimate=pl.CostEstimate(flops=flops, bytes_accessed=nbytes, transcendentals=0),
    )(*ins)


def shaped(shape, dtype):
    return jax.ShapeDtypeStruct(shape, dtype)


def head_of(tab, device):
    head = jnp.int32(-1)
    for d, h in enumerate(tab):
        if h >= 0:
            head = jnp.where(device == d, jnp.int32(h), head)
    return head


def head_at(me, tab, chips, half, c):
    return head_of(tab, me[0] ^ (half * chips + c))


def pack(me, tab, chips, source, mine, other):
    rows = source.shape[0]
    for half, out in ((0, mine), (1, other)):
        for c in range(chips):
            col = columns(jnp.maximum(head_at(me, tab, chips, half, c), 0))
            out[c * rows : (c + 1) * rows] = source[:, col]


def squares(ref):
    total = None
    for i in range(ref.shape[1] // HD):
        x = ref[:, tile(i)].astype(F32)
        total = x * x if total is None else total + x * x
    return total


def first_kernel(tab, chips, me, q_hbm, k_hbm, t_hbm, v_hbm, tv_hbm, mine, other, sums, q, k, t, v, sems):
    tokens = v_hbm.shape[0]
    copies = []
    pairs = [(v_hbm, v.at[:tokens]), (tv_hbm, v.at[tokens:]), (k_hbm, k), (q_hbm, q), (t_hbm, t)]
    for i, (a, b) in enumerate(pairs):
        copies.append(pltpu.make_async_copy(a, b, sems.at[i]))
        copies[-1].start()
    copies[0].wait()
    copies[1].wait()
    pack(me, tab, chips, v, mine, other)
    for copy in copies[2:]:
        copy.wait()
    parts = [squares(q), squares(k), squares(t)]
    rest = sums.shape[1] - sum(p.shape[0] for p in parts)
    if rest:
        parts.append(jnp.zeros((rest, HD), F32))
    sums[...] = rows_to_row(jnp.concatenate(parts, axis=0))


def merge_kernel(chips, mine, other, *outs):
    rows = mine.shape[0] // chips
    for c, out in enumerate(outs):
        out[:rows] = mine[c * rows : (c + 1) * rows]
        out[rows:] = other[c * rows : (c + 1) * rows]


def send_k_kernel(tab, width, count, chips, me, *refs):
    sums, (k, tk, gain, mine, other, scales, normed) = refs[:count], refs[count:]
    tokens, texts = k.shape[0], tk.shape[0]
    scale = lax.rsqrt(total_of(sums) * (1.0 / width) + EPS)
    scales[...] = scale
    cols = row_to_columns(scale[:, tokens:])
    for i in range(k.shape[1] // HD):
        g = gain[:, tile(i)]
        normed[:tokens, tile(i)] = (k[:, tile(i)].astype(F32) * cols[:tokens] * g).astype(BF)
        normed[tokens:, tile(i)] = (
            tk[:, tile(i)].astype(F32) * cols[tokens : tokens + texts] * g
        ).astype(BF)
    pack(me, tab, chips, normed, mine, other)


def send_q_kernel(tab, chips, me, vid, scales, q, gain, cot, mine, other, both):
    tokens = q.shape[0]
    cols = row_to_columns(scales[:, :tokens])
    row = me[0] * tokens + lax.broadcasted_iota(jnp.int32, (tokens, HD), 0)
    live = row < vid[0]
    for i in range(q.shape[1] // HD):
        g = gain[:, tile(i)]
        both[:tokens, tile(i)] = (q[:, tile(i)].astype(F32) * cols * g).astype(BF)
        both[tokens:, tile(i)] = jnp.where(live, cot[:, tile(i)].astype(F32), 0.0).astype(BF)
    pack(me, tab, chips, both, mine, other)


def places(members, tokens, texts, source):
    text_at = pl.ds(pl.multiple_of(source * texts, texts), texts)
    video_at = pl.ds(pl.multiple_of(members * texts + source * tokens, texts), tokens)
    return text_at, video_at


def assemble_kernel(chips, texts, me, *refs):
    pieces_v, pieces_k = refs[:chips], refs[chips : 2 * chips]
    k, v, kt, vt = refs[2 * chips :]
    span = pieces_v[0].shape[0] // 2
    tokens = span - texts
    for pieces, whole in ((pieces_k, k), (pieces_v, v)):
        for c in range(chips):
            for half in (0, 1):
                source = me[0] ^ (half * chips + c)
                text_at, video_at = places(2 * chips, tokens, texts, source)
                whole[text_at] = pieces[c][half * span + tokens : (half + 1) * span]
                whole[video_at] = pieces[c][half * span : half * span + tokens]
    for whole, turned in ((k, kt), (v, vt)):
        step = 256
        for start in range(0, whole.shape[0], step):
            turned[:, start : start + step] = whole[start : start + step, :].T


def attention_kernel(tab, spec, me, vid, txt, *refs):
    chips, tokens, texts, c, first, last, step = spec
    refs = list(refs)
    take = lambda count: [refs.pop(0) for _ in range(count)]
    (query,) = take(1)
    k, v, kt, vt = take(4)
    if not first:
        dk_in, dv_in, gain_in = take(3)
    (out,) = take(1)
    dk, dv, gains = take(3)
    if last:
        (dots,) = take(1)
    scores, weights, top, totals, turned_out, turned_dq = take(6)
    scale = HD ** (-0.5)
    span = 2 * chips * texts
    rows = k.shape[0]

    if first:
        dk[...] = jnp.zeros_like(dk)
        dv[...] = jnp.zeros_like(dv)
        gains[...] = jnp.zeros_like(gains)
    else:
        dk[...] = dk_in[...]
        dv[...] = dv_in[...]
        gains[...] = gain_in[...]

    blocks = span // step + (vid[0] + step - 1) // step

    def over_blocks(visit):
        def body(b, unused):
            start = pl.multiple_of(b * step, step)
            limit = jnp.where(start < span, txt[0] - start, vid[0] - (start - span))
            visit(pl.ds(start, step), limit)
            return unused

        lax.fori_loop(0, blocks, body, 0)

    def piece(half, unused):
        source = me[0] ^ (half * chips + c)
        active = jnp.logical_and(head_of(tab, me[0]) >= 0, source * tokens < vid[0])
        q_at = pl.ds(pl.multiple_of(half * 2 * tokens, tokens), tokens)
        grad_at = pl.ds(pl.multiple_of(half * 2 * tokens + tokens, tokens), tokens)

        @pl.when(jnp.logical_not(active))
        def _():
            out[q_at] = jnp.zeros((tokens, HD), BF)
            out[grad_at] = jnp.zeros((tokens, HD), BF)

        @pl.when(active)
        def _():
            q = query[q_at]
            grad = query[grad_at]
            top[...] = jnp.full_like(top, NEG)
            totals[...] = jnp.zeros_like(totals)
            turned_out[...] = jnp.zeros_like(turned_out)
            turned_dq[...] = jnp.zeros_like(turned_dq)

            def scan_scores(at, limit):
                s = nt(k[at], q)
                live = lax.broadcasted_iota(jnp.int32, s.shape, 0) < limit
                s = jnp.where(live, s, NEG)
                scores[at] = s
                top[...] = jnp.maximum(
                    top[...], jnp.max(s.reshape(step // 8, 8, tokens), axis=0)
                )

            over_blocks(scan_scores)
            highest = jnp.max(top[...], axis=0, keepdims=True) * (scale * LOG2E)

            def scan_weights(at, limit):
                p = jnp.exp2(scores[at] * (scale * LOG2E) - highest)
                totals[...] += jnp.sum(p.reshape(step // 8, 8, tokens), axis=0)
                low = p.astype(BF)
                weights[at] = low
                turned_out[...] += nn(vt[:, at], low)

            over_blocks(scan_weights)
            inverse = 1.0 / jnp.sum(totals[...], axis=0, keepdims=True)
            attention = turned_out[...] * inverse
            turned_grad = grad.astype(F32).T
            inner = jnp.sum(attention * turned_grad, axis=0, keepdims=True)
            inv_cols = row_to_columns(inverse)
            low_grad = (grad.astype(F32) * inv_cols).astype(BF)
            low_q = (q.astype(F32) * (inv_cols * scale)).astype(BF)
            out[q_at] = attention.T.astype(BF)

            def scan_grads(at, limit):
                p = weights[at]
                dp = nt(v[at], grad)
                ds = p * (dp - inner).astype(BF)
                dv[at] += nn(p, low_grad)
                dk[at] += nn(ds, low_q)
                turned_dq[...] += nn(kt[:, at], ds)

            over_blocks(scan_grads)
            dq = (turned_dq[...] * (inverse * scale)).T
            out[grad_at] = dq.astype(BF)
            part = dq * q.astype(F32)
            gains[...] += jnp.sum(part.reshape(tokens // 8, 8, HD), axis=0)

        return unused

    lax.fori_loop(0, 2, piece, 0)

    if last:
        for start in range(0, rows, step):
            at = slice(start, start + step)
            part = dk[at] * k[at].astype(F32)
            dots[:, at] = rows_to_row(part)
            gains_k = jnp.sum(part.reshape(step // 8, 8, HD), axis=0)
            if start == 0:
                top[:, :HD] = gains_k
            else:
                top[:, :HD] += gains_k
        gq = jnp.sum(gains[...], axis=0, keepdims=True)
        gk = jnp.sum(top[:, :HD], axis=0, keepdims=True)
        gains[...] = jnp.concatenate([gq, gk, jnp.zeros((6, HD), F32)], axis=0)


def split_rows(lines, rest):
    block = jnp.concatenate(lines, axis=0)
    high = block.astype(BF).astype(F32)
    both = [high, block - high]
    if rest:
        both.append(jnp.zeros((rest, HD), F32))
    return jnp.concatenate(both, axis=0).astype(BF)


def pack_v_kernel(chips, texts, me, dv, gains, *outs):
    span = outs[0].shape[0] // 2 - 16
    tokens = span - texts
    lines = split_rows([gains[0:1], gains[1:2]], 12)
    for c in range(chips):
        for half in (0, 1):
            source = me[0] ^ (half * chips + c)
            text_at, video_at = places(2 * chips, tokens, texts, source)
            base = half * (span + 16)
            outs[c][base : base + tokens] = dv[video_at].astype(BF)
            outs[c][base + tokens : base + span] = dv[text_at].astype(BF)
            outs[c][base + span : base + span + 16] = lines


def pack_k_kernel(chips, texts, count, me, dk, *refs):
    sums, outs, dots = refs[:count], refs[count:-1], refs[-1]
    dots[...] = total_of(sums)
    keys = dk.shape[0]
    text_total = 2 * chips * texts
    tokens = (keys - text_total) // (2 * chips)
    text_lines = [dots[:, tile(i)] for i in range(text_total // HD)]
    for c in range(chips):
        span = outs[c].shape[0] // 2
        for half in (0, 1):
            source = me[0] ^ (half * chips + c)
            text_at, video_at = places(2 * chips, tokens, texts, source)
            base = half * span
            outs[c][base : base + tokens] = dk[video_at].astype(BF)
            outs[c][base + tokens : base + tokens + texts] = dk[text_at].astype(BF)
            lines = list(text_lines)
            for i in range(tokens // HD):
                start = pl.multiple_of(text_total + source * tokens + i * HD, HD)
                lines.append(dots[:, pl.ds(start, HD)])
            rest = span - tokens - texts - 2 * len(lines)
            outs[c][base + tokens + texts : base + span] = split_rows(lines, rest)


def split_kernel(chips, *refs):
    out = refs[chips]
    rows = out.shape[0] // chips
    for c in range(chips):
        out[c * rows : (c + 1) * rows] = refs[c][rows:]


def each_head(me, tab, chips, blocks, other, visit):
    rows = other.shape[0] // chips
    for half in (0, 1):
        for c in range(chips):
            head = head_at(me, tab, chips, half, c)

            @pl.when(head >= 0)
            def _():
                col = columns(jnp.maximum(head, 0))
                if half:
                    visit(col, other, c * rows)
                else:
                    visit(col, blocks[c], 0)


def gather_q_kernel(tab, chips, me, vid, *refs):
    blocks, other = refs[:chips], refs[chips]
    q, gain, out, dq, dots = refs[chips + 1 :]
    tokens = q.shape[0]
    row = me[0] * tokens + lax.broadcasted_iota(jnp.int32, (tokens, HD), 0)
    live = row < vid[0]

    def visit(col, ref, at):
        o = ref[at : at + tokens].astype(F32)
        out[:, col] = jnp.where(live, o, 0.0).astype(BF)
        dq[:, col] = ref[at + tokens : at + 2 * tokens]

    each_head(me, tab, chips, blocks, other, visit)
    total = None
    for i in range(q.shape[1] // HD):
        term = q[:, tile(i)].astype(F32) * (dq[:, tile(i)].astype(F32) * gain[:, tile(i)])
        total = term if total is None else total + term
    dots[...] = rows_to_row(total)


def total_of(refs):
    total = refs[0][...]
    for ref in refs[1:]:
        total = total + ref[...]
    return total


def finish_q_kernel(width, count, *refs):
    dots = total_of(refs[:count])
    scales, q, dq, gain, out = refs[count:]
    scale = scales[:, : q.shape[0]]
    cols = row_to_columns(scale)
    back = row_to_columns(dots * (scale * scale * scale) * (1.0 / width))
    for i in range(q.shape[1] // HD):
        scaled = dq[:, tile(i)].astype(F32) * gain[:, tile(i)]
        out[:, tile(i)] = (cols * scaled - q[:, tile(i)].astype(F32) * back).astype(BF)


def gather_v_kernel(tab, chips, me, *refs):
    blocks, other = refs[:chips], refs[chips]
    q_gain, k_gain, out, text_out, dq_gain, dk_gain = refs[chips + 1 :]
    tokens, texts = out.shape[0], text_out.shape[0]

    def visit(col, ref, at):
        out[:, col] = ref[at : at + tokens]
        text_out[:, col] = ref[at + tokens : at + tokens + texts]
        lines = ref[at + tokens + texts : at + tokens + texts + 16].astype(F32)
        dq_gain[:, col] = (lines[0:1] + lines[2:3]) / q_gain[:, col]
        dk_gain[:, col] = (lines[1:2] + lines[3:4]) / k_gain[:, col]

    each_head(me, tab, chips, blocks, other, visit)


def finish_k_kernel(tab, width, chips, me, *refs):
    blocks, other = refs[:chips], refs[chips]
    scales, k, tk, k_gain = refs[chips + 1 : chips + 5]
    out, text_out, dk, sums, text_cols = refs[chips + 5 :]
    tokens, texts = k.shape[0], tk.shape[0]
    text_lines = 2 * chips * texts // HD
    lines = text_lines + tokens // HD
    sums[...] = jnp.zeros_like(sums)

    def visit(col, ref, at):
        dk[:, col] = ref[at : at + tokens + texts]
        block = ref[at + tokens + texts : at + tokens + texts + 2 * lines].astype(F32)
        block = block[:lines] + block[lines:]
        sums[:lines] += block

    each_head(me, tab, chips, blocks, other, visit)
    for i in range(text_lines):
        text_cols[i * HD : (i + 1) * HD] = row_to_columns(sums[i : i + 1])
    scale = scales[:, tokens:]
    cols = row_to_columns(scale)
    text_at = pl.ds(pl.multiple_of(me[0] * texts, texts), texts)
    dots = [row_to_columns(sums[text_lines + i : text_lines + 1 + i]) for i in range(tokens // HD)]
    dots.append(text_cols[text_at])
    rows = tokens + texts
    back = jnp.concatenate(dots, axis=0) * (cols[:rows] * cols[:rows]) * (1.0 / width)
    for i in range(k.shape[1] // HD):
        scaled = dk[:, tile(i)].astype(F32) * k_gain[:, tile(i)]
        scaled = cols[:rows] * scaled
        out[:, tile(i)] = (scaled[:tokens] - k[:, tile(i)].astype(F32) * back[:tokens]).astype(BF)
        text_out[:, tile(i)] = (
            scaled[tokens:] - tk[:, tile(i)].astype(F32) * back[tokens:]
        ).astype(BF)


def local(q_raw, k_raw, values, text_k, text_v, q_gain, k_gain, cotangent, vid_len, txt_len):
    tokens, cols = q_raw.shape
    texts = text_k.shape[0]
    heads = cols // HD
    chips = lax.axis_size("ctx")
    members = 2 * chips
    parts = lax.axis_size("tp")
    width = cols * parts
    table = head_owners(members, chips, heads)
    span = tokens + texts
    keys = members * span
    text_total = members * texts
    pad = -(-(2 * tokens + texts) // HD) * HD
    extra = -(-2 * (text_total // HD + tokens // HD) // 16) * 16

    me = lax.axis_index(GROUP).astype(jnp.int32).reshape(1)
    tab = tuple(int(h) for h in table)
    qg = q_gain.reshape(1, cols)
    kg = k_gain.reshape(1, cols)

    def along(block, c, to_owner):
        if c == 0:
            return block
        pairs = [(s, s ^ c) for s in range(members) if table[s ^ c if to_owner else s] >= 0]
        return lax.ppermute(block, GROUP, pairs)

    def sibling(block):
        return lax.ppermute(block, "section", [(0, 1), (1, 0)])

    def shared(block):
        got = [block]
        for d in range(1, parts):
            got.append(lax.ppermute(block, "tp", [(s, s ^ d) for s in range(parts)]))
        return got

    far_first = far_chips(chips)
    chip_order = [0] + far_first

    def merged(mine, other):
        rows = mine.shape[0] // chips
        messages = call(
            functools.partial(merge_kernel, chips),
            [shaped((2 * rows, HD), BF)] * chips,
            [mine, sibling(other)],
        )
        got = {c: along(messages[c], c, True) for c in far_first}
        got[0] = messages[0]
        return [got[c] for c in range(chips)]

    mine_v, other_v, sums = call(
        functools.partial(first_kernel, tab, chips),
        [shaped((chips * span, HD), BF)] * 2 + [shaped((1, pad), F32)],
        [me, q_raw, k_raw, text_k, values, text_v],
        smem=1,
        scratch=[
            pltpu.VMEM((tokens, cols), BF),
            pltpu.VMEM((tokens, cols), BF),
            pltpu.VMEM((texts, cols), BF),
            pltpu.VMEM((span, cols), BF),
            pltpu.SemaphoreType.DMA((5,)),
        ],
        space=pl.BlockSpec(memory_space=pltpu.HBM),
    )
    sums = shared(sums)
    got_v = merged(mine_v, other_v)
    mine_k, other_k, scales = call(
        functools.partial(send_k_kernel, tab, width, parts, chips),
        [shaped((chips * span, HD), BF)] * 2 + [shaped((1, pad), F32)],
        [me, *sums, k_raw, text_k, kg],
        smem=1,
        scratch=[pltpu.VMEM((span, cols), BF)],
    )
    got_k = merged(mine_k, other_k)
    mine_q, other_q = call(
        functools.partial(send_q_kernel, tab, chips),
        [shaped((chips * 2 * tokens, HD), BF)] * 2,
        [me, vid_len, scales, q_raw, qg, cotangent],
        smem=2,
        scratch=[pltpu.VMEM((2 * tokens, cols), BF)],
    )
    got_q = merged(mine_q, other_q)

    whole = call(
        functools.partial(assemble_kernel, chips, texts),
        [shaped((keys, HD), BF)] * 2 + [shaped((HD, keys), BF)] * 2,
        [me, *got_v, *got_k],
        smem=1,
    )

    carry = ()
    back_q = {}
    step = 512
    for i, c in enumerate(chip_order):
        first, last = i == 0, i == chips - 1
        outs = [shaped((4 * tokens, HD), BF)]
        outs += [shaped((keys, HD), F32)] * 2 + [shaped((8, HD), F32)]
        if last:
            outs.append(shaped((1, keys), F32))
        ins = [me, vid_len, txt_len, got_q[c], *whole, *carry]
        result = call(
            functools.partial(attention_kernel, tab, (chips, tokens, texts, c, first, last, step)),
            outs,
            ins,
            smem=3,
            scratch=[
                pltpu.VMEM((keys, tokens), F32),
                pltpu.VMEM((keys, tokens), BF),
                pltpu.VMEM((8, tokens), F32),
                pltpu.VMEM((8, tokens), F32),
                pltpu.VMEM((HD, tokens), F32),
                pltpu.VMEM((HD, tokens), F32),
            ],
            flops=6 * 2 * 2 * tokens * keys * HD * 2,
            aliases={} if first else {8: 1, 9: 2, 10: 3},
        )
        back_q[c] = along(result[0], c, False)
        carry = result[1:4]
    dk_sum, dv_sum, gains = carry
    dv_parts = call(
        functools.partial(pack_v_kernel, chips, texts),
        [shaped((2 * (span + 16), HD), BF)] * chips,
        [me, dv_sum, gains],
        smem=1,
    )
    back_v = {c: along(dv_parts[c], c, False) for c in far_first + [0]}
    dots = shared(result[4])
    dk_parts = call(
        functools.partial(pack_k_kernel, chips, texts, parts),
        [shaped((2 * (span + extra), HD), BF)] * chips,
        [me, dk_sum, *dots],
        smem=1,
        scratch=[pltpu.VMEM((1, keys), F32)],
    )
    back_k = {c: along(dk_parts[c], c, False) for c in far_first + [0]}

    def mine_and_other(back):
        blocks = [back[c] for c in range(chips)]
        rows = blocks[0].shape[0] // 2
        (other,) = call(
            functools.partial(split_kernel, chips), [shaped((chips * rows, HD), BF)], blocks
        )
        return [*blocks, sibling(other)]

    attention_out, dq, dots_q = call(
        functools.partial(gather_q_kernel, tab, chips),
        [shaped((tokens, cols), BF)] * 2 + [shaped((1, tokens), F32)],
        [me, vid_len, *mine_and_other(back_q), q_raw, qg],
        smem=2,
    )
    (d_q_raw,) = call(
        functools.partial(finish_q_kernel, width, parts),
        [shaped((tokens, cols), BF)],
        [*shared(dots_q), scales, q_raw, dq, qg],
    )
    d_values, d_text_v, d_q_gain, d_k_gain = call(
        functools.partial(gather_v_kernel, tab, chips),
        [shaped((tokens, cols), BF), shaped((texts, cols), BF)] + [shaped((1, cols), F32)] * 2,
        [me, *mine_and_other(back_v), qg, kg],
        smem=1,
    )
    d_k_raw, d_text_k = call(
        functools.partial(finish_k_kernel, tab, width, chips),
        [shaped((tokens, cols), BF), shaped((texts, cols), BF)],
        [me, *mine_and_other(back_k), scales, k_raw, text_k, kg],
        smem=1,
        scratch=[
            pltpu.VMEM((span, cols), BF),
            pltpu.VMEM((extra, HD), F32),
            pltpu.VMEM((text_total, HD), F32),
        ],
    )
    return (
        attention_out,
        d_q_raw,
        d_k_raw,
        d_values,
        d_text_k,
        d_text_v,
        d_q_gain.reshape(cols),
        d_k_gain.reshape(cols),
    )


def far_chips(chips):
    return sorted(range(1, chips), key=lambda c: (-c.bit_length(), c))


def solution(mesh):
    rows = P(GROUP, "tp")
    return jax.shard_map(
        local,
        mesh=mesh,
        in_specs=(rows,) * 5 + (P("tp"), P("tp"), rows, P(), P()),
        out_specs=(rows,) * 6 + (P("tp"), P("tp")),
        check_vma=False,
    )
```

profile of v0, /device:TPU:0, one launch (start us, length us, event | category | flops | bytes accessed | tf_op | source)
XLA Modules:
  0.0 149.2 jit_solution(16535784707033587844)
XLA Ops:
  5.5 1.3 shard_map.161
  7.3 3.5 %collective-permute-start.2 = (f32[1,640]{1,0:T(1,128)S(1)}, f32[1,640]{1,0:T(1,128)S(1)}, u32[]{:S(2)}, u32[]{:S(2)}) collective-permute-start(f32[1,640]{1,0:T(1,128)S(1)} %get-tuple-element.66.refs_0_), channel_id=1, source_target_pairs={{0,3},{1,2},{2,1},{3,0},{4,7},{5,6},{6,5},{7,4},{8,11},{9,10},{10,... | collective-permute-start | bytes 7688 | tf_op jit(solution)/shard_map/ppermute | solution.py:487
  12.4 2.0 %collective-permute-done.1.refs_2_ = f32[1,640]{1,0:T(1,128)S(1)} collective-permute-done((f32[1,640]{1,0:T(1,128)S(1)}, f32[1,640]{1,0:T(1,128)S(1)}, u32[]{:S(2)}, u32[]{:S(2)}) %collective-permute-start.1) | collective-permute-done | bytes 2592 | tf_op jit(solution)/shard_map/ppermute | solution.py:487
  16.6 3.5 %collective-permute-start.5 = (bf16[640,128]{1,0:T(8,128)(2,1)S(1)}, bf16[640,128]{1,0:T(8,128)(2,1)S(1)}, u32[]{:S(2)}, u32[]{:S(2)}) collective-permute-start(bf16[640,128]{1,0:T(8,128)(2,1)S(1)} %get-tuple-element.74), channel_id=1, source_target_pairs={{0,4},{4,0},{8,12},{12,8},{16,20},{28,24},{1,5},{5,1},{9,13},{13,9... | collective-permute-start | bytes 491528 | tf_op jit(solution)/shard_map/ppermute | solution.py:479
  20.1 4.5 %collective-permute-start.6 = (bf16[640,128]{1,0:T(8,128)(2,1)S(1)}, bf16[640,128]{1,0:T(8,128)(2,1)S(1)}, u32[]{:S(2)}, u32[]{:S(2)}) collective-permute-start(bf16[640,128]{1,0:T(8,128)(2,1)S(1)} %get-tuple-element.75), channel_id=1, source_target_pairs={{0,8},{4,12},{8,0},{12,4},{16,24},{28,20},{1,9},{5,13},{9,1},{13,5... | collective-permute-start | bytes 491528 | tf_op jit(solution)/shard_map/ppermute | solution.py:479
  24.6 2.1 %collective-permute-start.7 = (bf16[640,128]{1,0:T(8,128)(2,1)S(1)}, bf16[640,128]{1,0:T(8,128)(2,1)S(1)}, u32[]{:S(2)}, u32[]{:S(2)}) collective-permute-start(bf16[640,128]{1,0:T(8,128)(2,1)S(1)} %get-tuple-element.76), channel_id=1, source_target_pairs={{0,12},{4,8},{8,4},{12,0},{20,24},{24,20},{1,13},{5,9},{9,5},{13,1... | collective-permute-start | bytes 491528 | tf_op jit(solution)/shard_map/ppermute | solution.py:479
  26.8 2.6 %collective-permute-start.9 = (bf16[640,128]{1,0:T(8,128)(2,1)S(1)}, bf16[640,128]{1,0:T(8,128)(2,1)S(1)}, u32[]{:S(2)}, u32[]{:S(2)}) collective-permute-start(bf16[640,128]{1,0:T(8,128)(2,1)S(1)} %get-tuple-element.80), channel_id=1, source_target_pairs={{0,4},{4,0},{8,12},{12,8},{16,20},{28,24},{1,5},{5,1},{9,13},{13,9... | collective-permute-start | bytes 491528 | tf_op jit(solution)/shard_map/ppermute | solution.py:479
  29.4 5.4 %collective-permute-start.10 = (bf16[640,128]{1,0:T(8,128)(2,1)S(1)}, bf16[640,128]{1,0:T(8,128)(2,1)S(1)}, u32[]{:S(2)}, u32[]{:S(2)}) collective-permute-start(bf16[640,128]{1,0:T(8,128)(2,1)S(1)} %get-tuple-element.81), channel_id=1, source_target_pairs={{0,8},{4,12},{8,0},{12,4},{16,24},{28,20},{1,9},{5,13},{9,1},{13,5... | collective-permute-start | bytes 491528 | tf_op jit(solution)/shard_map/ppermute | solution.py:479
  34.8 5.6 %collective-permute-start.11 = (bf16[640,128]{1,0:T(8,128)(2,1)S(1)}, bf16[640,128]{1,0:T(8,128)(2,1)S(1)}, u32[]{:S(2)}, u32[]{:S(2)}) collective-permute-start(bf16[640,128]{1,0:T(8,128)(2,1)S(1)} %get-tuple-element.82), channel_id=1, source_target_pairs={{0,12},{4,8},{8,4},{12,0},{20,24},{24,20},{1,13},{5,9},{9,5},{13,1... | collective-permute-start | bytes 491528 | tf_op jit(solution)/shard_map/ppermute | solution.py:479
  41.1 3.0 %collective-permute-done.10.refs_6_ = bf16[640,128]{1,0:T(8,128)(2,1)S(1)} collective-permute-done((bf16[640,128]{1,0:T(8,128)(2,1)S(1)}, bf16[640,128]{1,0:T(8,128)(2,1)S(1)}, u32[]{:S(2)}, u32[]{:S(2)}) %collective-permute-start.10) | collective-permute-done | bytes 163872 | tf_op jit(solution)/shard_map/ppermute | solution.py:479
  44.6 4.2 %collective-permute-start.12 = (bf16[1024,128]{1,0:T(8,128)(2,1)S(1)}, bf16[1024,128]{1,0:T(8,128)(2,1)S(1)}, u32[]{:S(2)}, u32[]{:S(2)}) collective-permute-start(bf16[1024,128]{1,0:T(8,128)(2,1)S(1)} %get-tuple-element.88), channel_id=1, source_target_pairs={{0,4},{4,0},{8,12},{12,8},{16,20},{28,24},{1,5},{5,1},{9,13},{13,9... | collective-permute-start | bytes 786440 | tf_op jit(solution)/shard_map/ppermute | solution.py:479
  48.8 4.3 %collective-permute-start.13 = (bf16[1024,128]{1,0:T(8,128)(2,1)S(1)}, bf16[1024,128]{1,0:T(8,128)(2,1)S(1)}, u32[]{:S(2)}, u32[]{:S(2)}) collective-permute-start(bf16[1024,128]{1,0:T(8,128)(2,1)S(1)} %get-tuple-element.89), channel_id=1, source_target_pairs={{0,12},{4,8},{8,4},{12,0},{20,24},{24,20},{1,13},{5,9},{9,5},{13,1... | collective-permute-start | bytes 786440 | tf_op jit(solution)/shard_map/ppermute | solution.py:479
  53.2 1.9 %collective-permute-start.14 = (bf16[1024,128]{1,0:T(8,128)(2,1)S(1)}, bf16[1024,128]{1,0:T(8,128)(2,1)S(1)}, u32[]{:S(2)}, u32[]{:S(2)}) collective-permute-start(bf16[1024,128]{1,0:T(8,128)(2,1)S(1)} %get-tuple-element.90), channel_id=1, source_target_pairs={{0,8},{4,12},{8,0},{12,4},{16,24},{28,20},{1,9},{5,13},{9,1},{13,5... | collective-permute-start | bytes 786440 | tf_op jit(solution)/shard_map/ppermute | solution.py:479
  55.1 10.3 %shard_map.168 = (bf16[1024,128]{1,0:T(8,128)(2,1)S(1)}, f32[2560,128]{1,0:T(8,128)S(1)}, f32[2560,128]{1,0:T(8,128)S(1)}, f32[8,128]{1,0:T(8,128)S(1)}) custom-call(s32[1]{0:T(128)} %bitcast.me, s32[1]{0:T(128)S(6)} %copy.36.vid, s32[1]{0:T(128)S(6)} %copy.37.txt, bf16[1024,128]{1,0:T(8,128)(2,1)S(1)} %get-tuple-element.70.refs_0_, ...), custom_call_target="tpu_custom_call" | custom-call | flops 4026531840 | bytes 5771264 | tf_op jit(solution)/shard_map/pallas_call | solution.py:60
  65.4 10.4 %shard_map.169 = (bf16[1024,128]{1,0:T(8,128)(2,1)S(1)}, f32[2560,128]{1,0:T(8,128)S(1)}, f32[2560,128]{1,0:T(8,128)S(1)}, f32[8,128]{1,0:T(8,128)S(1)}) custom-call(s32[1]{0:T(128)} %bitcast.me, s32[1]{0:T(128)S(6)} %copy.36.vid, s32[1]{0:T(128)S(6)} %copy.37.txt, ...), custom_call_target="tpu_custom_call", output_to_operand_aliasing={{1}: (8, {}), {2}: (9, {}), {3}: (10, {})} | custom-call | flops 4026531840 | bytes 8396800 | tf_op jit(solution)/shard_map/pallas_call | solution.py:60
  75.9 10.4 %shard_map.170 = (bf16[1024,128]{1,0:T(8,128)(2,1)S(1)}, f32[2560,128]{1,0:T(8,128)S(1)}, f32[2560,128]{1,0:T(8,128)S(1)}, f32[8,128]{1,0:T(8,128)S(1)}) custom-call(s32[1]{0:T(128)} %bitcast.me, s32[1]{0:T(128)S(6)} %copy.36.vid, s32[1]{0:T(128)S(6)} %copy.37.txt, ...), custom_call_target="tpu_custom_call", output_to_operand_aliasing={{1}: (8, {}), {2}: (9, {}), {3}: (10, {})} | custom-call | flops 4026531840 | bytes 8396800 | tf_op jit(solution)/shard_map/pallas_call | solution.py:60
  86.3 10.9 %shard_map.171 = (bf16[1024,128]{1,0:T(8,128)(2,1)S(1)}, f32[2560,128]{1,0:T(8,128)S(1)}, f32[2560,128]{1,0:T(8,128)S(1)}, f32[8,128]{1,0:T(8,128)S(1)}, f32[1,2560]{1,0:T(1,128)S(1)}) custom-call(s32[1]{0:T(128)} %bitcast.me, s32[1]{0:T(128)S(6)} %copy.36.vid, s32[1]{0:T(128)S(6)} %copy.37.txt, ...), custom_call_target="tpu_custom_call", output_to_operand_aliasing={{1}: (8, {}), {2}: (9, {}), {3}: (10, {})} | custom-call | flops 4026531840 | bytes 8407040 | tf_op jit(solution)/shard_map/pallas_call | solution.py:60
  97.2 3.9 %collective-permute-start.15 = (bf16[1024,128]{1,0:T(8,128)(2,1)S(1)}, bf16[1024,128]{1,0:T(8,128)(2,1)S(1)}, u32[]{:S(2)}, u32[]{:S(2)}) collective-permute-start(bf16[1024,128]{1,0:T(8,128)(2,1)S(1)} %get-tuple-element.100), channel_id=1, source_target_pairs={{0,4},{4,0},{8,12},{12,8},{20,16},{24,28},{1,5},{5,1},{9,13},{13,9... | collective-permute-start | bytes 786440 | tf_op jit(solution)/shard_map/ppermute | solution.py:479
  101.1 4.3 %collective-permute-start.17 = (bf16[1024,128]{1,0:T(8,128)(2,1)S(1)}, bf16[1024,128]{1,0:T(8,128)(2,1)S(1)}, u32[]{:S(2)}, u32[]{:S(2)}) collective-permute-start(bf16[1024,128]{1,0:T(8,128)(2,1)S(1)} %get-tuple-element.102), channel_id=1, source_target_pairs={{0,12},{4,8},{8,4},{12,0},{20,24},{24,20},{1,13},{5,9},{9,5},{13,1... | collective-permute-start | bytes 786440 | tf_op jit(solution)/shard_map/ppermute | solution.py:479
  105.4 1.9 %collective-permute-start.16 = (bf16[1024,128]{1,0:T(8,128)(2,1)S(1)}, bf16[1024,128]{1,0:T(8,128)(2,1)S(1)}, u32[]{:S(2)}, u32[]{:S(2)}) collective-permute-start(bf16[1024,128]{1,0:T(8,128)(2,1)S(1)} %get-tuple-element.101), channel_id=1, source_target_pairs={{0,8},{4,12},{8,0},{12,4},{20,28},{24,16},{1,9},{5,13},{9,1},{13,5... | collective-permute-start | bytes 786440 | tf_op jit(solution)/shard_map/ppermute | solution.py:479
  107.4 3.9 %collective-permute-start.29 = (bf16[672,128]{1,0:T(8,128)(2,1)S(1)}, bf16[672,128]{1,0:T(8,128)(2,1)S(1)}, u32[]{:S(2)}, u32[]{:S(2)}) collective-permute-start(bf16[672,128]{1,0:T(8,128)(2,1)S(1)} %get-tuple-element.116), channel_id=1, source_target_pairs={{0,4},{4,0},{8,12},{12,8},{20,16},{24,28},{1,5},{5,1},{9,13},{13,9... | collective-permute-start | bytes 516104 | tf_op jit(solution)/shard_map/ppermute | solution.py:479
  111.3 2.9 %collective-permute-start.30 = (bf16[672,128]{1,0:T(8,128)(2,1)S(1)}, bf16[672,128]{1,0:T(8,128)(2,1)S(1)}, u32[]{:S(2)}, u32[]{:S(2)}) collective-permute-start(bf16[672,128]{1,0:T(8,128)(2,1)S(1)} %get-tuple-element.117), channel_id=1, source_target_pairs={{0,8},{4,12},{8,0},{12,4},{20,28},{24,16},{1,9},{5,13},{9,1},{13,5... | collective-permute-start | bytes 516104 | tf_op jit(solution)/shard_map/ppermute | solution.py:479
  114.2 1.6 %collective-permute-start.24 = (f32[1,2560]{1,0:T(1,128)S(1)}, f32[1,2560]{1,0:T(1,128)S(1)}, u32[]{:S(2)}, u32[]{:S(2)}) collective-permute-start(f32[1,2560]{1,0:T(1,128)S(1)} %get-tuple-element.107.refs_0_), channel_id=1, source_target_pairs={{0,3},{1,2},{2,1},{3,0},{4,7},{5,6},{6,5},{7,4},{8,11},{9,10},{10,... | collective-permute-start | bytes 30728 | tf_op jit(solution)/shard_map/ppermute | solution.py:487
  116.3 2.9 %collective-permute-done.16.refs_2_ = bf16[1024,128]{1,0:T(8,128)(2,1)S(1)} collective-permute-done((bf16[1024,128]{1,0:T(8,128)(2,1)S(1)}, bf16[1024,128]{1,0:T(8,128)(2,1)S(1)}, u32[]{:S(2)}, u32[]{:S(2)}) %collective-permute-start.16) | collective-permute-done | bytes 262176 | tf_op jit(solution)/shard_map/ppermute | solution.py:479
  119.9 4.6 %collective-permute-start.31 = (bf16[672,128]{1,0:T(8,128)(2,1)S(1)}, bf16[672,128]{1,0:T(8,128)(2,1)S(1)}, u32[]{:S(2)}, u32[]{:S(2)}) collective-permute-start(bf16[672,128]{1,0:T(8,128)(2,1)S(1)} %get-tuple-element.118), channel_id=1, source_target_pairs={{0,12},{4,8},{8,4},{12,0},{20,24},{24,20},{1,13},{5,9},{9,5},{13,1... | collective-permute-start | bytes 516104 | tf_op jit(solution)/shard_map/ppermute | solution.py:479
  124.6 1.9 %collective-permute-start.25 = (bf16[672,128]{1,0:T(8,128)(2,1)S(1)}, bf16[672,128]{1,0:T(8,128)(2,1)S(1)}, u32[]{:S(2)}, u32[]{:S(2)}) collective-permute-start(bf16[672,128]{1,0:T(8,128)(2,1)S(1)} %get-tuple-element.109), channel_id=1, source_target_pairs={{0,4},{4,0},{8,12},{12,8},{20,16},{24,28},{1,5},{5,1},{9,13},{13,9... | collective-permute-start | bytes 516104 | tf_op jit(solution)/shard_map/ppermute | solution.py:479
  126.5 3.5 %collective-permute-start.26 = (bf16[672,128]{1,0:T(8,128)(2,1)S(1)}, bf16[672,128]{1,0:T(8,128)(2,1)S(1)}, u32[]{:S(2)}, u32[]{:S(2)}) collective-permute-start(bf16[672,128]{1,0:T(8,128)(2,1)S(1)} %get-tuple-element.110), channel_id=1, source_target_pairs={{0,8},{4,12},{8,0},{12,4},{20,28},{24,16},{1,9},{5,13},{9,1},{13,5... | collective-permute-start | bytes 516104 | tf_op jit(solution)/shard_map/ppermute | solution.py:479
  130.1 4.6 %collective-permute-start.27 = (bf16[672,128]{1,0:T(8,128)(2,1)S(1)}, bf16[672,128]{1,0:T(8,128)(2,1)S(1)}, u32[]{:S(2)}, u32[]{:S(2)}) collective-permute-start(bf16[672,128]{1,0:T(8,128)(2,1)S(1)} %get-tuple-element.111), channel_id=1, source_target_pairs={{0,12},{4,8},{8,4},{12,0},{20,24},{24,20},{1,13},{5,9},{9,5},{13,1... | collective-permute-start | bytes 516104 | tf_op jit(solution)/shard_map/ppermute | solution.py:479
  134.9 5.1 %collective-permute-done.26.refs_2_ = bf16[672,128]{1,0:T(8,128)(2,1)S(1)} collective-permute-done((bf16[672,128]{1,0:T(8,128)(2,1)S(1)}, bf16[672,128]{1,0:T(8,128)(2,1)S(1)}, u32[]{:S(2)}, u32[]{:S(2)}) %collective-permute-start.26) | collective-permute-done | bytes 172064 | tf_op jit(solution)/shard_map/ppermute | solution.py:479
  141.3 1.7 %collective-permute-start.21 = (f32[1,256]{1,0:T(1,128)S(1)}, f32[1,256]{1,0:T(1,128)S(1)}, u32[]{:S(2)}, u32[]{:S(2)}) collective-permute-start(f32[1,256]{1,0:T(1,128)S(1)} %get-tuple-element.104.refs_0_), channel_id=1, source_target_pairs={{0,3},{1,2},{2,1},{3,0},{4,7},{5,6},{6,5},{7,4},{8,11},{9,10},{10,... | collective-permute-start | bytes 3080 | tf_op jit(solution)/shard_map/ppermute | solution.py:487
  143.5 1.3 collective-permute-start.19
  146.9 1.3 shard_map.177
  (80 shorter events, 15.2 us)
Async XLA Ops:
  6.7 9.8 %collective-permute-start.4 = (bf16[1280,128]{1,0:T(8,128)(2,1)S(1)}, bf16[1280,128]{1,0:T(8,128)(2,1)S(1)}, u32[]{:S(2)}, u32[]{:S(2)}) collective-permute-start(bf16[1280,128]{1,0:T(8,128)(2,1)S(1)} %get-tuple-element.72), channel_id=1, source_target_pairs={{0,16},{16,0},{1,17},{17,1},{2,18},{18,2},{3,19},{19,3},{4,20},{20... | collective-permute-start | bytes 983048 | tf_op jit(solution)/shard_map/ppermute | solution.py:482
  7.3 5.1 %collective-permute-start.2 = (f32[1,640]{1,0:T(1,128)S(1)}, f32[1,640]{1,0:T(1,128)S(1)}, u32[]{:S(2)}, u32[]{:S(2)}) collective-permute-start(f32[1,640]{1,0:T(1,128)S(1)} %get-tuple-element.66.refs_0_), channel_id=1, source_target_pairs={{0,3},{1,2},{2,1},{3,0},{4,7},{5,6},{6,5},{7,4},{8,11},{9,10},{10,... | collective-permute-start | bytes 7688 | tf_op jit(solution)/shard_map/ppermute | solution.py:487
  10.8 3.6 %collective-permute-start.1 = (f32[1,640]{1,0:T(1,128)S(1)}, f32[1,640]{1,0:T(1,128)S(1)}, u32[]{:S(2)}, u32[]{:S(2)}) collective-permute-start(f32[1,640]{1,0:T(1,128)S(1)} %get-tuple-element.66.refs_0_), channel_id=1, source_target_pairs={{0,2},{1,3},{2,0},{3,1},{4,6},{5,7},{6,4},{7,5},{8,10},{9,11},{10,... | collective-permute-start | bytes 7688 | tf_op jit(solution)/shard_map/ppermute | solution.py:487
  16.0 28.6 %collective-permute-start.3 = (bf16[2048,128]{1,0:T(8,128)(2,1)S(1)}, bf16[2048,128]{1,0:T(8,128)(2,1)S(1)}, u32[]{:S(2)}, u32[]{:S(2)}) collective-permute-start(bf16[2048,128]{1,0:T(8,128)(2,1)S(1)} %get-tuple-element.69), channel_id=1, source_target_pairs={{0,16},{16,0},{1,17},{17,1},{2,18},{18,2},{3,19},{19,3},{4,20},{20... | collective-permute-start | bytes 1572872 | tf_op jit(solution)/shard_map/ppermute | solution.py:482
  16.0 10.7 %collective-permute-start.8 = (bf16[1280,128]{1,0:T(8,128)(2,1)S(1)}, bf16[1280,128]{1,0:T(8,128)(2,1)S(1)}, u32[]{:S(2)}, u32[]{:S(2)}) collective-permute-start(bf16[1280,128]{1,0:T(8,128)(2,1)S(1)} %get-tuple-element.78), channel_id=1, source_target_pairs={{0,16},{16,0},{1,17},{17,1},{2,18},{18,2},{3,19},{19,3},{4,20},{20... | collective-permute-start | bytes 983048 | tf_op jit(solution)/shard_map/ppermute | solution.py:482
  16.6 12.8 %collective-permute-start.5 = (bf16[640,128]{1,0:T(8,128)(2,1)S(1)}, bf16[640,128]{1,0:T(8,128)(2,1)S(1)}, u32[]{:S(2)}, u32[]{:S(2)}) collective-permute-start(bf16[640,128]{1,0:T(8,128)(2,1)S(1)} %get-tuple-element.74), channel_id=1, source_target_pairs={{0,4},{4,0},{8,12},{12,8},{16,20},{28,24},{1,5},{5,1},{9,13},{13,9... | collective-permute-start | bytes 491528 | tf_op jit(solution)/shard_map/ppermute | solution.py:479
  20.1 14.7 %collective-permute-start.6 = (bf16[640,128]{1,0:T(8,128)(2,1)S(1)}, bf16[640,128]{1,0:T(8,128)(2,1)S(1)}, u32[]{:S(2)}, u32[]{:S(2)}) collective-permute-start(bf16[640,128]{1,0:T(8,128)(2,1)S(1)} %get-tuple-element.75), channel_id=1, source_target_pairs={{0,8},{4,12},{8,0},{12,4},{16,24},{28,20},{1,9},{5,13},{9,1},{13,5... | collective-permute-start | bytes 491528 | tf_op jit(solution)/shard_map/ppermute | solution.py:479
  24.6 16.5 %collective-permute-start.7 = (bf16[640,128]{1,0:T(8,128)(2,1)S(1)}, bf16[640,128]{1,0:T(8,128)(2,1)S(1)}, u32[]{:S(2)}, u32[]{:S(2)}) collective-permute-start(bf16[640,128]{1,0:T(8,128)(2,1)S(1)} %get-tuple-element.76), channel_id=1, source_target_pairs={{0,12},{4,8},{8,4},{12,0},{20,24},{24,20},{1,13},{5,9},{9,5},{13,1... | collective-permute-start | bytes 491528 | tf_op jit(solution)/shard_map/ppermute | solution.py:479
  26.8 14.3 %collective-permute-start.9 = (bf16[640,128]{1,0:T(8,128)(2,1)S(1)}, bf16[640,128]{1,0:T(8,128)(2,1)S(1)}, u32[]{:S(2)}, u32[]{:S(2)}) collective-permute-start(bf16[640,128]{1,0:T(8,128)(2,1)S(1)} %get-tuple-element.80), channel_id=1, source_target_pairs={{0,4},{4,0},{8,12},{12,8},{16,20},{28,24},{1,5},{5,1},{9,13},{13,9... | collective-permute-start | bytes 491528 | tf_op jit(solution)/shard_map/ppermute | solution.py:479
  29.4 14.7 %collective-permute-start.10 = (bf16[640,128]{1,0:T(8,128)(2,1)S(1)}, bf16[640,128]{1,0:T(8,128)(2,1)S(1)}, u32[]{:S(2)}, u32[]{:S(2)}) collective-permute-start(bf16[640,128]{1,0:T(8,128)(2,1)S(1)} %get-tuple-element.81), channel_id=1, source_target_pairs={{0,8},{4,12},{8,0},{12,4},{16,24},{28,20},{1,9},{5,13},{9,1},{13,5... | collective-permute-start | bytes 491528 | tf_op jit(solution)/shard_map/ppermute | solution.py:479
  34.8 9.3 %collective-permute-start.11 = (bf16[640,128]{1,0:T(8,128)(2,1)S(1)}, bf16[640,128]{1,0:T(8,128)(2,1)S(1)}, u32[]{:S(2)}, u32[]{:S(2)}) collective-permute-start(bf16[640,128]{1,0:T(8,128)(2,1)S(1)} %get-tuple-element.82), channel_id=1, source_target_pairs={{0,12},{4,8},{8,4},{12,0},{20,24},{24,20},{1,13},{5,9},{9,5},{13,1... | collective-permute-start | bytes 491528 | tf_op jit(solution)/shard_map/ppermute | solution.py:479
  44.6 41.7 %collective-permute-start.12 = (bf16[1024,128]{1,0:T(8,128)(2,1)S(1)}, bf16[1024,128]{1,0:T(8,128)(2,1)S(1)}, u32[]{:S(2)}, u32[]{:S(2)}) collective-permute-start(bf16[1024,128]{1,0:T(8,128)(2,1)S(1)} %get-tuple-element.88), channel_id=1, source_target_pairs={{0,4},{4,0},{8,12},{12,8},{16,20},{28,24},{1,5},{5,1},{9,13},{13,9... | collective-permute-start | bytes 786440 | tf_op jit(solution)/shard_map/ppermute | solution.py:479
  48.8 27.0 %collective-permute-start.13 = (bf16[1024,128]{1,0:T(8,128)(2,1)S(1)}, bf16[1024,128]{1,0:T(8,128)(2,1)S(1)}, u32[]{:S(2)}, u32[]{:S(2)}) collective-permute-start(bf16[1024,128]{1,0:T(8,128)(2,1)S(1)} %get-tuple-element.89), channel_id=1, source_target_pairs={{0,12},{4,8},{8,4},{12,0},{20,24},{24,20},{1,13},{5,9},{9,5},{13,1... | collective-permute-start | bytes 786440 | tf_op jit(solution)/shard_map/ppermute | solution.py:479
  53.2 12.2 %collective-permute-start.14 = (bf16[1024,128]{1,0:T(8,128)(2,1)S(1)}, bf16[1024,128]{1,0:T(8,128)(2,1)S(1)}, u32[]{:S(2)}, u32[]{:S(2)}) collective-permute-start(bf16[1024,128]{1,0:T(8,128)(2,1)S(1)} %get-tuple-element.90), channel_id=1, source_target_pairs={{0,8},{4,12},{8,0},{12,4},{16,24},{28,20},{1,9},{5,13},{9,1},{13,5... | collective-permute-start | bytes 786440 | tf_op jit(solution)/shard_map/ppermute | solution.py:479
  97.2 17.0 %collective-permute-start.15 = (bf16[1024,128]{1,0:T(8,128)(2,1)S(1)}, bf16[1024,128]{1,0:T(8,128)(2,1)S(1)}, u32[]{:S(2)}, u32[]{:S(2)}) collective-permute-start(bf16[1024,128]{1,0:T(8,128)(2,1)S(1)} %get-tuple-element.100), channel_id=1, source_target_pairs={{0,4},{4,0},{8,12},{12,8},{20,16},{24,28},{1,5},{5,1},{9,13},{13,9... | collective-permute-start | bytes 786440 | tf_op jit(solution)/shard_map/ppermute | solution.py:479
  101.1 14.7 %collective-permute-start.17 = (bf16[1024,128]{1,0:T(8,128)(2,1)S(1)}, bf16[1024,128]{1,0:T(8,128)(2,1)S(1)}, u32[]{:S(2)}, u32[]{:S(2)}) collective-permute-start(bf16[1024,128]{1,0:T(8,128)(2,1)S(1)} %get-tuple-element.102), channel_id=1, source_target_pairs={{0,12},{4,8},{8,4},{12,0},{20,24},{24,20},{1,13},{5,9},{9,5},{13,1... | collective-permute-start | bytes 786440 | tf_op jit(solution)/shard_map/ppermute | solution.py:479
  105.4 13.7 %collective-permute-start.16 = (bf16[1024,128]{1,0:T(8,128)(2,1)S(1)}, bf16[1024,128]{1,0:T(8,128)(2,1)S(1)}, u32[]{:S(2)}, u32[]{:S(2)}) collective-permute-start(bf16[1024,128]{1,0:T(8,128)(2,1)S(1)} %get-tuple-element.101), channel_id=1, source_target_pairs={{0,8},{4,12},{8,0},{12,4},{20,28},{24,16},{1,9},{5,13},{9,1},{13,5... | collective-permute-start | bytes 786440 | tf_op jit(solution)/shard_map/ppermute | solution.py:479
  107.4 19.1 %collective-permute-start.29 = (bf16[672,128]{1,0:T(8,128)(2,1)S(1)}, bf16[672,128]{1,0:T(8,128)(2,1)S(1)}, u32[]{:S(2)}, u32[]{:S(2)}) collective-permute-start(bf16[672,128]{1,0:T(8,128)(2,1)S(1)} %get-tuple-element.116), channel_id=1, source_target_pairs={{0,4},{4,0},{8,12},{12,8},{20,16},{24,28},{1,5},{5,1},{9,13},{13,9... | collective-permute-start | bytes 516104 | tf_op jit(solution)/shard_map/ppermute | solution.py:479
  111.3 18.8 %collective-permute-start.30 = (bf16[672,128]{1,0:T(8,128)(2,1)S(1)}, bf16[672,128]{1,0:T(8,128)(2,1)S(1)}, u32[]{:S(2)}, u32[]{:S(2)}) collective-permute-start(bf16[672,128]{1,0:T(8,128)(2,1)S(1)} %get-tuple-element.117), channel_id=1, source_target_pairs={{0,8},{4,12},{8,0},{12,4},{20,28},{24,16},{1,9},{5,13},{9,1},{13,5... | collective-permute-start | bytes 516104 | tf_op jit(solution)/shard_map/ppermute | solution.py:479
  114.2 5.5 %collective-permute-start.24 = (f32[1,2560]{1,0:T(1,128)S(1)}, f32[1,2560]{1,0:T(1,128)S(1)}, u32[]{:S(2)}, u32[]{:S(2)}) collective-permute-start(f32[1,2560]{1,0:T(1,128)S(1)} %get-tuple-element.107.refs_0_), channel_id=1, source_target_pairs={{0,3},{1,2},{2,1},{3,0},{4,7},{5,6},{6,5},{7,4},{8,11},{9,10},{10,... | collective-permute-start | bytes 30728 | tf_op jit(solution)/shard_map/ppermute | solution.py:487
  115.8 4.1 %collective-permute-start.23 = (f32[1,2560]{1,0:T(1,128)S(1)}, f32[1,2560]{1,0:T(1,128)S(1)}, u32[]{:S(2)}, u32[]{:S(2)}) collective-permute-start(f32[1,2560]{1,0:T(1,128)S(1)} %get-tuple-element.107.refs_0_), channel_id=1, source_target_pairs={{0,2},{1,3},{2,0},{3,1},{4,6},{5,7},{6,4},{7,5},{8,10},{9,11},{10,... | collective-permute-start | bytes 30728 | tf_op jit(solution)/shard_map/ppermute | solution.py:487
  119.2 5.3 %collective-permute-start.22 = (f32[1,2560]{1,0:T(1,128)S(1)}, f32[1,2560]{1,0:T(1,128)S(1)}, u32[]{:S(2)}, u32[]{:S(2)}) collective-permute-start(f32[1,2560]{1,0:T(1,128)S(1)} %get-tuple-element.107.refs_0_), channel_id=1, source_target_pairs={{0,1},{1,0},{2,3},{3,2},{4,5},{5,4},{6,7},{7,6},{8,9},{9,8},{10,11... | collective-permute-start | bytes 30728 | tf_op jit(solution)/shard_map/ppermute | solution.py:487
  119.8 20.4 %collective-permute-start.18 = (bf16[2048,128]{1,0:T(8,128)(2,1)S(1)}, bf16[2048,128]{1,0:T(8,128)(2,1)S(1)}, u32[]{:S(2)}, u32[]{:S(2)}) collective-permute-start(bf16[2048,128]{1,0:T(8,128)(2,1)S(1)} %shard_map.172), channel_id=1, source_target_pairs={{0,16},{16,0},{1,17},{17,1},{2,18},{18,2},{3,19},{19,3},{4,20},{20... | collective-permute-start | bytes 1572872 | tf_op jit(solution)/shard_map/ppermute | solution.py:482
  119.9 14.9 %collective-permute-start.31 = (bf16[672,128]{1,0:T(8,128)(2,1)S(1)}, bf16[672,128]{1,0:T(8,128)(2,1)S(1)}, u32[]{:S(2)}, u32[]{:S(2)}) collective-permute-start(bf16[672,128]{1,0:T(8,128)(2,1)S(1)} %get-tuple-element.118), channel_id=1, source_target_pairs={{0,12},{4,8},{8,4},{12,0},{20,24},{24,20},{1,13},{5,9},{9,5},{13,1... | collective-permute-start | bytes 516104 | tf_op jit(solution)/shard_map/ppermute | solution.py:479
  124.6 10.3 %collective-permute-start.25 = (bf16[672,128]{1,0:T(8,128)(2,1)S(1)}, bf16[672,128]{1,0:T(8,128)(2,1)S(1)}, u32[]{:S(2)}, u32[]{:S(2)}) collective-permute-start(bf16[672,128]{1,0:T(8,128)(2,1)S(1)} %get-tuple-element.109), channel_id=1, source_target_pairs={{0,4},{4,0},{8,12},{12,8},{20,16},{24,28},{1,5},{5,1},{9,13},{13,9... | collective-permute-start | bytes 516104 | tf_op jit(solution)/shard_map/ppermute | solution.py:479
  126.5 13.5 %collective-permute-start.26 = (bf16[672,128]{1,0:T(8,128)(2,1)S(1)}, bf16[672,128]{1,0:T(8,128)(2,1)S(1)}, u32[]{:S(2)}, u32[]{:S(2)}) collective-permute-start(bf16[672,128]{1,0:T(8,128)(2,1)S(1)} %get-tuple-element.110), channel_id=1, source_target_pairs={{0,8},{4,12},{8,0},{12,4},{20,28},{24,16},{1,9},{5,13},{9,1},{13,5... | collective-permute-start | bytes 516104 | tf_op jit(solution)/shard_map/ppermute | solution.py:479
  130.1 9.9 %collective-permute-start.27 = (bf16[672,128]{1,0:T(8,128)(2,1)S(1)}, bf16[672,128]{1,0:T(8,128)(2,1)S(1)}, u32[]{:S(2)}, u32[]{:S(2)}) collective-permute-start(bf16[672,128]{1,0:T(8,128)(2,1)S(1)} %get-tuple-element.111), channel_id=1, source_target_pairs={{0,12},{4,8},{8,4},{12,0},{20,24},{24,20},{1,13},{5,9},{9,5},{13,1... | collective-permute-start | bytes 516104 | tf_op jit(solution)/shard_map/ppermute | solution.py:479
  134.8 10.0 %collective-permute-start.32 = (bf16[1344,128]{1,0:T(8,128)(2,1)S(1)}, bf16[1344,128]{1,0:T(8,128)(2,1)S(1)}, u32[]{:S(2)}, u32[]{:S(2)}) collective-permute-start(bf16[1344,128]{1,0:T(8,128)(2,1)S(1)} %shard_map.179), channel_id=1, source_target_pairs={{0,16},{16,0},{1,17},{17,1},{2,18},{18,2},{3,19},{19,3},{4,20},{20... | collective-permute-start | bytes 1032200 | tf_op jit(solution)/shard_map/ppermute | solution.py:482
  140.1 6.9 %collective-permute-start.28 = (bf16[1344,128]{1,0:T(8,128)(2,1)S(1)}, bf16[1344,128]{1,0:T(8,128)(2,1)S(1)}, u32[]{:S(2)}, u32[]{:S(2)}) collective-permute-start(bf16[1344,128]{1,0:T(8,128)(2,1)S(1)} %shard_map.176), channel_id=1, source_target_pairs={{0,16},{16,0},{1,17},{17,1},{2,18},{18,2},{3,19},{19,3},{4,20},{20... | collective-permute-start | bytes 1032200 | tf_op jit(solution)/shard_map/ppermute | solution.py:482
  141.3 7.0 %collective-permute-start.21 = (f32[1,256]{1,0:T(1,128)S(1)}, f32[1,256]{1,0:T(1,128)S(1)}, u32[]{:S(2)}, u32[]{:S(2)}) collective-permute-start(f32[1,256]{1,0:T(1,128)S(1)} %get-tuple-element.104.refs_0_), channel_id=1, source_target_pairs={{0,3},{1,2},{2,1},{3,0},{4,7},{5,6},{6,5},{7,4},{8,11},{9,10},{10,... | collective-permute-start | bytes 3080 | tf_op jit(solution)/shard_map/ppermute | solution.py:487
  143.0 5.2 %collective-permute-start.20 = (f32[1,256]{1,0:T(1,128)S(1)}, f32[1,256]{1,0:T(1,128)S(1)}, u32[]{:S(2)}, u32[]{:S(2)}) collective-permute-start(f32[1,256]{1,0:T(1,128)S(1)} %get-tuple-element.104.refs_0_), channel_id=1, source_target_pairs={{0,2},{1,3},{2,0},{3,1},{4,6},{5,7},{6,4},{7,5},{8,10},{9,11},{10,... | collective-permute-start | bytes 3080 | tf_op jit(solution)/shard_map/ppermute | solution.py:487
  143.5 4.7 %collective-permute-start.19 = (f32[1,256]{1,0:T(1,128)S(1)}, f32[1,256]{1,0:T(1,128)S(1)}, u32[]{:S(2)}, u32[]{:S(2)}) collective-permute-start(f32[1,256]{1,0:T(1,128)S(1)} %get-tuple-element.104.refs_0_), channel_id=1, source_target_pairs={{0,1},{1,0},{2,3},{3,2},{4,5},{5,4},{6,7},{7,6},{8,9},{9,8},{10,11... | collective-permute-start | bytes 3080 | tf_op jit(solution)/shard_map/ppermute | solution.py:487
  (12 other events, 70.1 us)
where the time goes:
time: 150 us; the launch traced here: 149 us
  starting transfers between devices  77.4 us (52%)
  Pallas kernels  49.5 us (33%)
  waiting for transfers between devices  13.9 us (9%)
  local copies, waits for them, and re-layouts  4.8 us (3%)
  between operations  2.45 us (2%)
    ppermute x18, starting transfers between devices, along(): return lax.ppermute(block, GROUP, pairs)  65.8 us
    pallas_call x20, Pallas kernels, call(): pl.pallas_call(kernel, out_shape=tuple((jax.ShapeDtypeStruct(o.shape, o.d...  49.5 us
    ppermute x18, waiting for transfers between devices, along(): return lax.ppermute(block, GROUP, pairs)  11.1 us
    ppermute x9, starting transfers between devices, shared(): got.append(lax.ppermute(block, 'tp', [(s, s ^ d) for s in range(parts)]))  10.2 us
    unnamed x22, local copies, waits for them, and re-layouts  4.79 us
  transfers between devices with their start and end apart: 33, of which 6 were waited for; matrix products, arithmetic and copies ran while one was open for 1% of the time, Pallas kernels for 24%

commit v1 on v0

--- a/solution.py
+++ b/solution.py
@@ -178,42 +178,35 @@
             turned[:, start : start + step] = whole[start : start + step, :].T
 
 
-def attention_kernel(tab, spec, me, vid, txt, *refs):
-    chips, tokens, texts, c, first, last, step = spec
-    refs = list(refs)
-    take = lambda count: [refs.pop(0) for _ in range(count)]
-    (query,) = take(1)
-    k, v, kt, vt = take(4)
-    if not first:
-        dk_in, dv_in, gain_in = take(3)
-    (out,) = take(1)
-    dk, dv, gains = take(3)
-    if last:
-        (dots,) = take(1)
-    scores, weights, top, totals, turned_out, turned_dq = take(6)
+def attention_kernel(tab, spec, me, vid, txt, query, k, v, kt, vt, *refs):
+    chips, tokens, texts, c, step = spec
+    out, dk, dv, gains, scores, weights, top, totals, turned_out, turned_dq = refs
     scale = HD ** (-0.5)
     span = 2 * chips * texts
     rows = k.shape[0]
-
-    if first:
-        dk[...] = jnp.zeros_like(dk)
-        dv[...] = jnp.zeros_like(dv)
-        gains[...] = jnp.zeros_like(gains)
-    else:
-        dk[...] = dk_in[...]
-        dv[...] = dv_in[...]
-        gains[...] = gain_in[...]
-
-    blocks = span // step + (vid[0] + step - 1) // step
-
-    def over_blocks(visit):
-        def body(b, unused):
-            start = pl.multiple_of(b * step, step)
-            limit = jnp.where(start < span, txt[0] - start, vid[0] - (start - span))
-            visit(pl.ds(start, step), limit)
-            return unused
-
-        lax.fori_loop(0, blocks, body, 0)
+    videos = rows - span
+    blocks = [slice(start, start + step) for start in range(0, rows, step)]
+    low_text, low_video = span * 3 // 4, span + videos // 2
+
+    gains[...] = jnp.zeros_like(gains)
+
+    def masked(s, start):
+        parts = []
+        for begin, end, limit in (
+            (0, low_text, None),
+            (low_text, span, txt[0]),
+            (span, low_video, None),
+            (low_video, rows, span + vid[0]),
+        ):
+            begin, end = max(begin, start), min(end, start + step)
+            if begin >= end:
+                continue
+            part = s[begin - start : end - start]
+            if limit is not None:
+                row = lax.broadcasted_iota(jnp.int32, part.shape, 0)
+                part = jnp.where(row < limit - begin, part, NEG)
+            parts.append(part)
+        return parts[0] if len(parts) == 1 else jnp.concatenate(parts, axis=0)
 
     def piece(half, unused):
         source = me[0] ^ (half * chips + c)
@@ -226,35 +219,28 @@
             out[q_at] = jnp.zeros((tokens, HD), BF)
             out[grad_at] = jnp.zeros((tokens, HD), BF)
 
-        @pl.when(active)
-        def _():
+            @pl.when(half == 0)
+            def _():
+                dk[...] = jnp.zeros_like(dk)
+                dv[...] = jnp.zeros_like(dv)
+
+        def work(add):
             q = query[q_at]
             grad = query[grad_at]
-            top[...] = jnp.full_like(top, NEG)
-            totals[...] = jnp.zeros_like(totals)
-            turned_out[...] = jnp.zeros_like(turned_out)
-            turned_dq[...] = jnp.zeros_like(turned_dq)
-
-            def scan_scores(at, limit):
-                s = nt(k[at], q)
-                live = lax.broadcasted_iota(jnp.int32, s.shape, 0) < limit
-                s = jnp.where(live, s, NEG)
+            for i, at in enumerate(blocks):
+                s = masked(nt(k[at], q), at.start)
                 scores[at] = s
-                top[...] = jnp.maximum(
-                    top[...], jnp.max(s.reshape(step // 8, 8, tokens), axis=0)
-                )
-
-            over_blocks(scan_scores)
+                most = jnp.max(s.reshape(step // 8, 8, tokens), axis=0)
+                top[...] = most if i == 0 else jnp.maximum(top[...], most)
             highest = jnp.max(top[...], axis=0, keepdims=True) * (scale * LOG2E)
-
-            def scan_weights(at, limit):
+            for i, at in enumerate(blocks):
                 p = jnp.exp2(scores[at] * (scale * LOG2E) - highest)
-                totals[...] += jnp.sum(p.reshape(step // 8, 8, tokens), axis=0)
+                part = jnp.sum(p.reshape(step // 8, 8, tokens), axis=0)
                 low = p.astype(BF)
                 weights[at] = low
-                turned_out[...] += nn(vt[:, at], low)
-
-            over_blocks(scan_weights)
+                o = nn(vt[:, at], low)
+                totals[...] = part if i == 0 else totals[...] + part
+                turned_out[...] = o if i == 0 else turned_out[...] + o
             inverse = 1.0 / jnp.sum(totals[...], axis=0, keepdims=True)
             attention = turned_out[...] * inverse
             turned_grad = grad.astype(F32).T
@@ -263,38 +249,38 @@
             low_grad = (grad.astype(F32) * inv_cols).astype(BF)
             low_q = (q.astype(F32) * (inv_cols * scale)).astype(BF)
             out[q_at] = attention.T.astype(BF)
-
-            def scan_grads(at, limit):
+            for i, at in enumerate(blocks):
                 p = weights[at]
                 dp = nt(v[at], grad)
                 ds = p * (dp - inner).astype(BF)
-                dv[at] += nn(p, low_grad)
-                dk[at] += nn(ds, low_q)
-                turned_dq[...] += nn(kt[:, at], ds)
-
-            over_blocks(scan_grads)
+                dv_part, dk_part = nn(p, low_grad), nn(ds, low_q)
+                dv[at] = jnp.where(add, dv[at], 0.0) + dv_part
+                dk[at] = jnp.where(add, dk[at], 0.0) + dk_part
+                dq = nn(kt[:, at], ds)
+                turned_dq[...] = dq if i == 0 else turned_dq[...] + dq
             dq = (turned_dq[...] * (inverse * scale)).T
             out[grad_at] = dq.astype(BF)
             part = dq * q.astype(F32)
             gains[...] += jnp.sum(part.reshape(tokens // 8, 8, HD), axis=0)
 
+        @pl.when(active)
+        def _():
+            work(half > 0)
+
         return unused
 
     lax.fori_loop(0, 2, piece, 0)
 
-    if last:
-        for start in range(0, rows, step):
-            at = slice(start, start + step)
-            part = dk[at] * k[at].astype(F32)
-            dots[:, at] = rows_to_row(part)
-            gains_k = jnp.sum(part.reshape(step // 8, 8, HD), axis=0)
-            if start == 0:
-                top[:, :HD] = gains_k
-            else:
-                top[:, :HD] += gains_k
-        gq = jnp.sum(gains[...], axis=0, keepdims=True)
-        gk = jnp.sum(top[:, :HD], axis=0, keepdims=True)
-        gains[...] = jnp.concatenate([gq, gk, jnp.zeros((6, HD), F32)], axis=0)
+
+def attention_scratch(keys, tokens):
+    return [
+        pltpu.VMEM((keys, tokens), F32),
+        pltpu.VMEM((keys, tokens), BF),
+        pltpu.VMEM((8, tokens), F32),
+        pltpu.VMEM((8, tokens), F32),
+        pltpu.VMEM((HD, tokens), F32),
+        pltpu.VMEM((HD, tokens), F32),
+    ]
 
 
 def split_rows(lines, rest):
@@ -306,17 +292,31 @@
     return jnp.concatenate(both, axis=0).astype(BF)
 
 
-def pack_v_kernel(chips, texts, me, dv, gains, *outs):
+def pack_v_kernel(chips, texts, me, k, *refs):
+    dks, dvs, gains = refs[:chips], refs[chips : 2 * chips], refs[2 * chips : 3 * chips]
+    outs, dk, dots, dv = refs[3 * chips : 4 * chips], refs[4 * chips], refs[4 * chips + 1], refs[-1]
     span = outs[0].shape[0] // 2 - 16
     tokens = span - texts
-    lines = split_rows([gains[0:1], gains[1:2]], 12)
+    rows, step = k.shape[0], 512
+    gk = jnp.zeros((8, HD), F32)
+    for start in range(0, rows, step):
+        at = slice(start, min(start + step, rows))
+        total = functools.reduce(lambda a, b: a + b, [ref[at] for ref in dks])
+        dk[at] = total
+        part = total * k[at].astype(F32)
+        dots[:, at] = rows_to_row(part)
+        gk = gk + jnp.sum(part.reshape(part.shape[0] // 8, 8, HD), axis=0)
+        dv[at] = functools.reduce(lambda a, b: a + b, [ref[at] for ref in dvs]).astype(BF)
+    gq = functools.reduce(lambda a, b: a + b, [ref[...] for ref in gains])
+    gq = jnp.sum(gq, axis=0, keepdims=True)
+    lines = split_rows([gq, jnp.sum(gk, axis=0, keepdims=True)], 12)
     for c in range(chips):
         for half in (0, 1):
             source = me[0] ^ (half * chips + c)
             text_at, video_at = places(2 * chips, tokens, texts, source)
             base = half * (span + 16)
-            outs[c][base : base + tokens] = dv[video_at].astype(BF)
-            outs[c][base + tokens : base + span] = dv[text_at].astype(BF)
+            outs[c][base : base + tokens] = dv[video_at]
+            outs[c][base + tokens : base + span] = dv[text_at]
             outs[c][base + span : base + span + 16] = lines
 
 
@@ -514,6 +514,7 @@
             pltpu.SemaphoreType.DMA((5,)),
         ],
         space=pl.BlockSpec(memory_space=pltpu.HBM),
+        vmem=60,
     )
     sums = shared(sums)
     got_v = merged(mine_v, other_v)
@@ -541,43 +542,34 @@
         smem=1,
     )
 
-    carry = ()
     back_q = {}
-    step = 512
-    for i, c in enumerate(chip_order):
-        first, last = i == 0, i == chips - 1
-        outs = [shaped((4 * tokens, HD), BF)]
-        outs += [shaped((keys, HD), F32)] * 2 + [shaped((8, HD), F32)]
-        if last:
-            outs.append(shaped((1, keys), F32))
-        ins = [me, vid_len, txt_len, got_q[c], *whole, *carry]
-        result = call(
-            functools.partial(attention_kernel, tab, (chips, tokens, texts, c, first, last, step)),
-            outs,
-            ins,
+    dk_calls, dv_calls, gain_calls = [], [], []
+    step = max(d for d in range(256, 1281, 128) if keys % d == 0)
+    for c in chip_order:
+        block, dk_call, dv_call, gain_call = call(
+            functools.partial(attention_kernel, tab, (chips, tokens, texts, c, step)),
+            [shaped((4 * tokens, HD), BF)]
+            + [shaped((keys, HD), F32)] * 2
+            + [shaped((8, HD), F32)],
+            [me, vid_len, txt_len, got_q[c], *whole],
             smem=3,
-            scratch=[
-                pltpu.VMEM((keys, tokens), F32),
-                pltpu.VMEM((keys, tokens), BF),
-                pltpu.VMEM((8, tokens), F32),
-                pltpu.VMEM((8, tokens), F32),
-                pltpu.VMEM((HD, tokens), F32),
-                pltpu.VMEM((HD, tokens), F32),
-            ],
+            scratch=attention_scratch(keys, tokens),
             flops=6 * 2 * 2 * tokens * keys * HD * 2,
-            aliases={} if first else {8: 1, 9: 2, 10: 3},
         )
-        back_q[c] = along(result[0], c, False)
-        carry = result[1:4]
-    dk_sum, dv_sum, gains = carry
-    dv_parts = call(
+        back_q[c] = along(block, c, False)
+        dk_calls.append(dk_call)
+        dv_calls.append(dv_call)
+        gain_calls.append(gain_call)
+    *dv_parts, dk_sum, dots = call(
         functools.partial(pack_v_kernel, chips, texts),
-        [shaped((2 * (span + 16), HD), BF)] * chips,
-        [me, dv_sum, gains],
+        [shaped((2 * (span + 16), HD), BF)] * chips
+        + [shaped((keys, HD), F32), shaped((1, keys), F32)],
+        [me, whole[0], *dk_calls, *dv_calls, *gain_calls],
         smem=1,
+        scratch=[pltpu.VMEM((keys, HD), BF)],
     )
     back_v = {c: along(dv_parts[c], c, False) for c in far_first + [0]}
-    dots = shared(result[4])
+    dots = shared(dots)
     dk_parts = call(
         functools.partial(pack_k_kernel, chips, texts, parts),
         [shaped((2 * (span + extra), HD), BF)] * chips,

time: 150 us -> 136 us (0.907)
  Pallas kernels: 49.5 us -> 31 us
  waiting for transfers between devices: 13.9 us -> 25.9 us
  local copies, waits for them, and re-layouts: 4.8 us -> 0.72 us
  starting transfers between devices: 77.4 us -> 73.6 us
    pallas_call x20, Pallas kernels: 49.5 us -> 31 us  [call(): pl.pallas_call(kernel, out_shape=tuple((jax.ShapeDtypeStruct(o.shape, o.d...]
    ppermute x18, waiting for transfers between devices: 11.1 us -> 19.5 us  [along(): return lax.ppermute(block, GROUP, pairs)]
    ppermute x18, starting transfers between devices: 65.8 us -> 61.2 us  [along(): return lax.ppermute(block, GROUP, pairs)]
    unnamed x22 -> x16, local copies, waits for them, and re-layouts: 4.79 us -> 0.72 us
    ppermute x9, waiting for transfers between devices: 2.77 us -> 4.61 us  [shared(): got.append(lax.ppermute(block, 'tp', [(s, s ^ d) for s in range(parts)]))]
    ppermute x6, waiting for transfers between devices: 0.02 us -> 1.8 us  [sibling(): return lax.ppermute(block, 'section', [(0, 1), (1, 0)])]
  transfers between devices with their start and end apart: 33 -> 33, of which waited for: 6 -> 11; matrix products, arithmetic and copies ran while one was open for 1% -> 1% of each run, Pallas kernels for 24% -> 20%
where the time goes in v1:
time: 136 us; the launch traced here: 135 us
  starting transfers between devices  73.6 us (54%)
  Pallas kernels  31 us (23%)
  waiting for transfers between devices  25.9 us (19%)
  between operations  2.44 us (2%)
    ppermute x18, starting transfers between devices, along(): return lax.ppermute(block, GROUP, pairs)  61.2 us
    pallas_call x20, Pallas kernels, call(): pl.pallas_call(kernel, out_shape=tuple((jax.ShapeDtypeStruct(o.shape, o.d...  31 us
    ppermute x18, waiting for transfers between devices, along(): return lax.ppermute(block, GROUP, pairs)  19.5 us
    ppermute x9, starting transfers between devices, shared(): got.append(lax.ppermute(block, 'tp', [(s, s ^ d) for s in range(parts)]))  11.7 us
    ppermute x9, waiting for transfers between devices, shared(): got.append(lax.ppermute(block, 'tp', [(s, s ^ d) for s in range(parts)]))  4.61 us
  transfers between devices with their start and end apart: 33, of which 11 were waited for; matrix products, arithmetic and copies ran while one was open for 1% of the time, Pallas kernels for 20%

profile of v1, /device:TPU:0, one launch (start us, length us, event | category | flops | bytes accessed | tf_op | source)
XLA Modules:
  0.0 135.0 jit_solution(4149347986733437759)
XLA Ops:
  0.7 2.3 %shard_map.161 = (bf16[1280,128]{1,0:T(8,128)(2,1)}, bf16[1280,128]{1,0:T(8,128)(2,1)}, f32[1,640]{1,0:T(1,128)}) custom-call(s32[1]{0:T(128)} %bitcast.me, bf16[256,768]{1,0:T(8,128)(2,1)} %refs_5_.5, bf16[256,768]{1,0:T(8,128)(2,1)} %refs_6_.1, bf16[64,768]{1,0:T(8,128)(2,1)} %refs_7_.1, bf16[256,768]{1,0:T(8,128)(2,1)} %v_hbm.1, bf16[64,768]{1,0:T(8,128)(2,1)} %tv_hbm.1), custom_call_target="tpu_custom_call" | custom-call | bytes 2034176 | tf_op jit(solution)/shard_map/pallas_call | solution.py:60
  3.0 4.0 %collective-permute-start.2 = (f32[1,640]{1,0:T(1,128)}, f32[1,640]{1,0:T(1,128)S(1)}, u32[]{:S(2)}, u32[]{:S(2)}) collective-permute-start(f32[1,640]{1,0:T(1,128)} %get-tuple-element.67.refs_0_), channel_id=1, source_target_pairs={{0,3},{1,2},{2,1},{3,0},{4,7},{5,6},{6,5},{7,4},{8,11},{9,10},{10,... | collective-permute-start | bytes 7688 | tf_op jit(solution)/shard_map/ppermute | solution.py:487
  8.8 2.0 %collective-permute-done.1.refs_2_ = f32[1,640]{1,0:T(1,128)S(1)} collective-permute-done((f32[1,640]{1,0:T(1,128)}, f32[1,640]{1,0:T(1,128)S(1)}, u32[]{:S(2)}, u32[]{:S(2)}) %collective-permute-start.1) | collective-permute-done | bytes 2592 | tf_op jit(solution)/shard_map/ppermute | solution.py:487
  13.7 1.8 %collective-permute-done.4.other = bf16[1280,128]{1,0:T(8,128)(2,1)S(1)} collective-permute-done((bf16[1280,128]{1,0:T(8,128)(2,1)}, bf16[1280,128]{1,0:T(8,128)(2,1)S(1)}, u32[]{:S(2)}, u32[]{:S(2)}) %collective-permute-start.4) | collective-permute-done | bytes 327712 | tf_op jit(solution)/shard_map/ppermute | solution.py:482
  15.5 3.5 %collective-permute-start.5 = (bf16[640,128]{1,0:T(8,128)(2,1)S(1)}, bf16[640,128]{1,0:T(8,128)(2,1)S(1)}, u32[]{:S(2)}, u32[]{:S(2)}) collective-permute-start(bf16[640,128]{1,0:T(8,128)(2,1)S(1)} %get-tuple-element.75), channel_id=1, source_target_pairs={{0,4},{4,0},{8,12},{12,8},{16,20},{28,24},{1,5},{5,1},{9,13},{13,9... | collective-permute-start | bytes 491528 | tf_op jit(solution)/shard_map/ppermute | solution.py:479
  19.0 4.5 %collective-permute-start.6 = (bf16[640,128]{1,0:T(8,128)(2,1)S(1)}, bf16[640,128]{1,0:T(8,128)(2,1)S(1)}, u32[]{:S(2)}, u32[]{:S(2)}) collective-permute-start(bf16[640,128]{1,0:T(8,128)(2,1)S(1)} %get-tuple-element.76), channel_id=1, source_target_pairs={{0,8},{4,12},{8,0},{12,4},{16,24},{28,20},{1,9},{5,13},{9,1},{13,5... | collective-permute-start | bytes 491528 | tf_op jit(solution)/shard_map/ppermute | solution.py:479
  23.6 2.1 %collective-permute-start.16 = (bf16[1024,128]{1,0:T(8,128)(2,1)S(1)}, bf16[1024,128]{1,0:T(8,128)(2,1)S(1)}, u32[]{:S(2)}, u32[]{:S(2)}) collective-permute-start(bf16[1024,128]{1,0:T(8,128)(2,1)S(1)} %get-tuple-element.93), channel_id=1, source_target_pairs={{0,12},{4,8},{8,4},{12,0},{20,24},{24,20},{1,13},{5,9},{9,5},{13,1... | collective-permute-start | bytes 786440 | tf_op jit(solution)/shard_map/ppermute | solution.py:479
  25.7 5.5 %collective-permute-start.7 = (bf16[640,128]{1,0:T(8,128)(2,1)S(1)}, bf16[640,128]{1,0:T(8,128)(2,1)S(1)}, u32[]{:S(2)}, u32[]{:S(2)}) collective-permute-start(bf16[640,128]{1,0:T(8,128)(2,1)S(1)} %get-tuple-element.77), channel_id=1, source_target_pairs={{0,12},{4,8},{8,4},{12,0},{20,24},{24,20},{1,13},{5,9},{9,5},{13,1... | collective-permute-start | bytes 491528 | tf_op jit(solution)/shard_map/ppermute | solution.py:479
  31.3 1.9 %collective-permute-start.9 = (bf16[640,128]{1,0:T(8,128)(2,1)S(1)}, bf16[640,128]{1,0:T(8,128)(2,1)S(1)}, u32[]{:S(2)}, u32[]{:S(2)}) collective-permute-start(bf16[640,128]{1,0:T(8,128)(2,1)S(1)} %get-tuple-element.81), channel_id=1, source_target_pairs={{0,4},{4,0},{8,12},{12,8},{16,20},{28,24},{1,5},{5,1},{9,13},{13,9... | collective-permute-start | bytes 491528 | tf_op jit(solution)/shard_map/ppermute | solution.py:479
  33.3 2.7 %collective-permute-start.10 = (bf16[640,128]{1,0:T(8,128)(2,1)S(1)}, bf16[640,128]{1,0:T(8,128)(2,1)S(1)}, u32[]{:S(2)}, u32[]{:S(2)}) collective-permute-start(bf16[640,128]{1,0:T(8,128)(2,1)S(1)} %get-tuple-element.82), channel_id=1, source_target_pairs={{0,8},{4,12},{8,0},{12,4},{16,24},{28,20},{1,9},{5,13},{9,1},{13,5... | collective-permute-start | bytes 491528 | tf_op jit(solution)/shard_map/ppermute | solution.py:479
  35.9 2.6 %collective-permute-done.6.refs_2_ = bf16[640,128]{1,0:T(8,128)(2,1)S(1)} collective-permute-done((bf16[640,128]{1,0:T(8,128)(2,1)S(1)}, bf16[640,128]{1,0:T(8,128)(2,1)S(1)}, u32[]{:S(2)}, u32[]{:S(2)}) %collective-permute-start.6) | collective-permute-done | bytes 163872 | tf_op jit(solution)/shard_map/ppermute | solution.py:479
  38.5 3.8 %collective-permute-start.11 = (bf16[640,128]{1,0:T(8,128)(2,1)S(1)}, bf16[640,128]{1,0:T(8,128)(2,1)S(1)}, u32[]{:S(2)}, u32[]{:S(2)}) collective-permute-start(bf16[640,128]{1,0:T(8,128)(2,1)S(1)} %get-tuple-element.83), channel_id=1, source_target_pairs={{0,12},{4,8},{8,4},{12,0},{20,24},{24,20},{1,13},{5,9},{9,5},{13,1... | collective-permute-start | bytes 491528 | tf_op jit(solution)/shard_map/ppermute | solution.py:479
  43.0 8.6 %collective-permute-done.10.refs_6_ = bf16[640,128]{1,0:T(8,128)(2,1)S(1)} collective-permute-done((bf16[640,128]{1,0:T(8,128)(2,1)S(1)}, bf16[640,128]{1,0:T(8,128)(2,1)S(1)}, u32[]{:S(2)}, u32[]{:S(2)}) %collective-permute-start.10) | collective-permute-done | bytes 163872 | tf_op jit(solution)/shard_map/ppermute | solution.py:479
  52.0 4.2 %collective-permute-start.12 = (bf16[1024,128]{1,0:T(8,128)(2,1)S(1)}, bf16[1024,128]{1,0:T(8,128)(2,1)S(1)}, u32[]{:S(2)}, u32[]{:S(2)}) collective-permute-start(bf16[1024,128]{1,0:T(8,128)(2,1)S(1)} %get-tuple-element.89), channel_id=1, source_target_pairs={{0,4},{4,0},{8,12},{12,8},{16,20},{28,24},{1,5},{5,1},{9,13},{13,9... | collective-permute-start | bytes 786440 | tf_op jit(solution)/shard_map/ppermute | solution.py:479
  56.3 2.9 %collective-permute-start.14 = (bf16[1024,128]{1,0:T(8,128)(2,1)S(1)}, bf16[1024,128]{1,0:T(8,128)(2,1)S(1)}, u32[]{:S(2)}, u32[]{:S(2)}) collective-permute-start(bf16[1024,128]{1,0:T(8,128)(2,1)S(1)} %get-tuple-element.91), channel_id=1, source_target_pairs={{0,8},{4,12},{8,0},{12,4},{16,24},{28,20},{1,9},{5,13},{9,1},{13,5... | collective-permute-start | bytes 786440 | tf_op jit(solution)/shard_map/ppermute | solution.py:479
  59.2 5.4 %shard_map.171 = (bf16[1024,128]{1,0:T(8,128)(2,1)S(1)}, f32[2560,128]{1,0:T(8,128)S(1)}, f32[2560,128]{1,0:T(8,128)S(1)}, f32[8,128]{1,0:T(8,128)S(1)}) custom-call(s32[1]{0:T(128)} %bitcast.me, s32[1]{0:T(128)S(6)} %copy.18.vid, s32[1]{0:T(128)S(6)} %copy.19.txt, bf16[1024,128]{1,0:T(8,128)(2,1)S(1)} %collective-permute-done.16.query, ...), custom_call_target="tpu_custom_call" | custom-call | flops 4026531840 | bytes 5771264 | tf_op jit(solution)/shard_map/pallas_call | solution.py:60
  64.6 3.4 %collective-permute-start.17 = (bf16[1024,128]{1,0:T(8,128)(2,1)S(1)}, bf16[1024,128]{1,0:T(8,128)(2,1)S(1)}, u32[]{:S(2)}, u32[]{:S(2)}) collective-permute-start(bf16[1024,128]{1,0:T(8,128)(2,1)S(1)} %get-tuple-element.94), channel_id=1, source_target_pairs={{0,12},{4,8},{8,4},{12,0},{20,24},{24,20},{1,13},{5,9},{9,5},{13,1... | collective-permute-start | bytes 786440 | tf_op jit(solution)/shard_map/ppermute | solution.py:479
  68.0 3.0 %collective-permute-done.14.query = bf16[1024,128]{1,0:T(8,128)(2,1)S(1)} collective-permute-done((bf16[1024,128]{1,0:T(8,128)(2,1)S(1)}, bf16[1024,128]{1,0:T(8,128)(2,1)S(1)}, u32[]{:S(2)}, u32[]{:S(2)}) %collective-permute-start.14) | collective-permute-done | bytes 262176 | tf_op jit(solution)/shard_map/ppermute | solution.py:479
  71.0 5.5 %shard_map.170 = (bf16[1024,128]{1,0:T(8,128)(2,1)S(1)}, f32[2560,128]{1,0:T(8,128)S(1)}, f32[2560,128]{1,0:T(8,128)S(1)}, f32[8,128]{1,0:T(8,128)S(1)}) custom-call(s32[1]{0:T(128)} %bitcast.me, s32[1]{0:T(128)S(6)} %copy.18.vid, s32[1]{0:T(128)S(6)} %copy.19.txt, bf16[1024,128]{1,0:T(8,128)(2,1)S(1)} %collective-permute-done.14.query, ...), custom_call_target="tpu_custom_call" | custom-call | flops 4026531840 | bytes 5771264 | tf_op jit(solution)/shard_map/pallas_call | solution.py:60
  76.5 1.9 %collective-permute-start.15 = (bf16[1024,128]{1,0:T(8,128)(2,1)S(1)}, bf16[1024,128]{1,0:T(8,128)(2,1)S(1)}, u32[]{:S(2)}, u32[]{:S(2)}) collective-permute-start(bf16[1024,128]{1,0:T(8,128)(2,1)S(1)} %get-tuple-element.92), channel_id=1, source_target_pairs={{0,8},{4,12},{8,0},{12,4},{20,28},{24,16},{1,9},{5,13},{9,1},{13,5... | collective-permute-start | bytes 786440 | tf_op jit(solution)/shard_map/ppermute | solution.py:479
  78.5 5.5 %shard_map.169 = (bf16[1024,128]{1,0:T(8,128)(2,1)S(1)}, f32[2560,128]{1,0:T(8,128)S(1)}, f32[2560,128]{1,0:T(8,128)S(1)}, f32[8,128]{1,0:T(8,128)S(1)}) custom-call(s32[1]{0:T(128)} %bitcast.me, s32[1]{0:T(128)S(6)} %copy.18.vid, s32[1]{0:T(128)S(6)} %copy.19.txt, bf16[1024,128]{1,0:T(8,128)(2,1)S(1)} %collective-permute-done.12.query, ...), custom_call_target="tpu_custom_call" | custom-call | flops 4026531840 | bytes 5771264 | tf_op jit(solution)/shard_map/pallas_call | solution.py:60
  83.9 4.6 %collective-permute-start.13 = (bf16[1024,128]{1,0:T(8,128)(2,1)S(1)}, bf16[1024,128]{1,0:T(8,128)(2,1)S(1)}, u32[]{:S(2)}, u32[]{:S(2)}) collective-permute-start(bf16[1024,128]{1,0:T(8,128)(2,1)S(1)} %get-tuple-element.90), channel_id=1, source_target_pairs={{0,4},{4,0},{8,12},{12,8},{20,16},{24,28},{1,5},{5,1},{9,13},{13,9... | collective-permute-start | bytes 786440 | tf_op jit(solution)/shard_map/ppermute | solution.py:479
  88.5 5.5 %shard_map.168 = (bf16[1024,128]{1,0:T(8,128)(2,1)S(1)}, f32[2560,128]{1,0:T(8,128)S(1)}, f32[2560,128]{1,0:T(8,128)S(1)}, f32[8,128]{1,0:T(8,128)S(1)}) custom-call(s32[1]{0:T(128)} %bitcast.me, s32[1]{0:T(128)S(6)} %copy.18.vid, s32[1]{0:T(128)S(6)} %copy.19.txt, bf16[1024,128]{1,0:T(8,128)(2,1)S(1)} %get-tuple-element.71.query, ...), custom_call_target="tpu_custom_call" | custom-call | flops 4026531840 | bytes 5771264 | tf_op jit(solution)/shard_map/pallas_call | solution.py:60
  94.8 1.9 %collective-permute-start.29 = (bf16[672,128]{1,0:T(8,128)(2,1)S(1)}, bf16[672,128]{1,0:T(8,128)(2,1)S(1)}, u32[]{:S(2)}, u32[]{:S(2)}) collective-permute-start(bf16[672,128]{1,0:T(8,128)(2,1)S(1)} %get-tuple-element.118), channel_id=1, source_target_pairs={{0,4},{4,0},{8,12},{12,8},{20,16},{24,28},{1,5},{5,1},{9,13},{13,9... | collective-permute-start | bytes 516104 | tf_op jit(solution)/shard_map/ppermute | solution.py:479
  96.7 4.3 %collective-permute-start.30 = (bf16[672,128]{1,0:T(8,128)(2,1)S(1)}, bf16[672,128]{1,0:T(8,128)(2,1)S(1)}, u32[]{:S(2)}, u32[]{:S(2)}) collective-permute-start(bf16[672,128]{1,0:T(8,128)(2,1)S(1)} %get-tuple-element.119), channel_id=1, source_target_pairs={{0,8},{4,12},{8,0},{12,4},{20,28},{24,16},{1,9},{5,13},{9,1},{13,5... | collective-permute-start | bytes 516104 | tf_op jit(solution)/shard_map/ppermute | solution.py:479
  101.1 1.6 %collective-permute-start.24 = (f32[1,2560]{1,0:T(1,128)S(1)}, f32[1,2560]{1,0:T(1,128)S(1)}, u32[]{:S(2)}, u32[]{:S(2)}) collective-permute-start(f32[1,2560]{1,0:T(1,128)S(1)} %get-tuple-element.111.refs_0_), channel_id=1, source_target_pairs={{0,3},{1,2},{2,1},{3,0},{4,7},{5,6},{6,5},{7,4},{8,11},{9,10},{10,... | collective-permute-start | bytes 30728 | tf_op jit(solution)/shard_map/ppermute | solution.py:487
  106.3 3.8 %collective-permute-start.31 = (bf16[672,128]{1,0:T(8,128)(2,1)S(1)}, bf16[672,128]{1,0:T(8,128)(2,1)S(1)}, u32[]{:S(2)}, u32[]{:S(2)}) collective-permute-start(bf16[672,128]{1,0:T(8,128)(2,1)S(1)} %get-tuple-element.120), channel_id=1, source_target_pairs={{0,12},{4,8},{8,4},{12,0},{20,24},{24,20},{1,13},{5,9},{9,5},{13,1... | collective-permute-start | bytes 516104 | tf_op jit(solution)/shard_map/ppermute | solution.py:479
  110.3 1.9 %collective-permute-start.25 = (bf16[672,128]{1,0:T(8,128)(2,1)S(1)}, bf16[672,128]{1,0:T(8,128)(2,1)S(1)}, u32[]{:S(2)}, u32[]{:S(2)}) collective-permute-start(bf16[672,128]{1,0:T(8,128)(2,1)S(1)} %get-tuple-element.113), channel_id=1, source_target_pairs={{0,4},{4,0},{8,12},{12,8},{20,16},{24,28},{1,5},{5,1},{9,13},{13,9... | collective-permute-start | bytes 516104 | tf_op jit(solution)/shard_map/ppermute | solution.py:479
  112.2 4.4 %collective-permute-start.26 = (bf16[672,128]{1,0:T(8,128)(2,1)S(1)}, bf16[672,128]{1,0:T(8,128)(2,1)S(1)}, u32[]{:S(2)}, u32[]{:S(2)}) collective-permute-start(bf16[672,128]{1,0:T(8,128)(2,1)S(1)} %get-tuple-element.114), channel_id=1, source_target_pairs={{0,8},{4,12},{8,0},{12,4},{20,28},{24,16},{1,9},{5,13},{9,1},{13,5... | collective-permute-start | bytes 516104 | tf_op jit(solution)/shard_map/ppermute | solution.py:479
  116.6 3.8 %collective-permute-start.27 = (bf16[672,128]{1,0:T(8,128)(2,1)S(1)}, bf16[672,128]{1,0:T(8,128)(2,1)S(1)}, u32[]{:S(2)}, u32[]{:S(2)}) collective-permute-start(bf16[672,128]{1,0:T(8,128)(2,1)S(1)} %get-tuple-element.115), channel_id=1, source_target_pairs={{0,12},{4,8},{8,4},{12,0},{20,24},{24,20},{1,13},{5,9},{9,5},{13,1... | collective-permute-start | bytes 516104 | tf_op jit(solution)/shard_map/ppermute | solution.py:479
  120.5 2.6 %collective-permute-done.26.refs_2_ = bf16[672,128]{1,0:T(8,128)(2,1)S(1)} collective-permute-done((bf16[672,128]{1,0:T(8,128)(2,1)S(1)}, bf16[672,128]{1,0:T(8,128)(2,1)S(1)}, u32[]{:S(2)}, u32[]{:S(2)}) %collective-permute-start.26) | collective-permute-done | bytes 172064 | tf_op jit(solution)/shard_map/ppermute | solution.py:479
  123.1 2.7 %collective-permute-done.27.refs_3_ = bf16[672,128]{1,0:T(8,128)(2,1)S(1)} collective-permute-done((bf16[672,128]{1,0:T(8,128)(2,1)S(1)}, bf16[672,128]{1,0:T(8,128)(2,1)S(1)}, u32[]{:S(2)}, u32[]{:S(2)}) %collective-permute-start.27) | collective-permute-done | bytes 172064 | tf_op jit(solution)/shard_map/ppermute | solution.py:479
  (74 shorter events, 18.4 us)
Async XLA Ops:
  3.0 5.8 %collective-permute-start.2 = (f32[1,640]{1,0:T(1,128)}, f32[1,640]{1,0:T(1,128)S(1)}, u32[]{:S(2)}, u32[]{:S(2)}) collective-permute-start(f32[1,640]{1,0:T(1,128)} %get-tuple-element.67.refs_0_), channel_id=1, source_target_pairs={{0,3},{1,2},{2,1},{3,0},{4,7},{5,6},{6,5},{7,4},{8,11},{9,10},{10,... | collective-permute-start | bytes 7688 | tf_op jit(solution)/shard_map/ppermute | solution.py:487
  7.0 3.8 %collective-permute-start.1 = (f32[1,640]{1,0:T(1,128)}, f32[1,640]{1,0:T(1,128)S(1)}, u32[]{:S(2)}, u32[]{:S(2)}) collective-permute-start(f32[1,640]{1,0:T(1,128)} %get-tuple-element.67.refs_0_), channel_id=1, source_target_pairs={{0,2},{1,3},{2,0},{3,1},{4,6},{5,7},{6,4},{7,5},{8,10},{9,11},{10,... | collective-permute-start | bytes 7688 | tf_op jit(solution)/shard_map/ppermute | solution.py:487
  7.5 3.8 %collective-permute-start = (f32[1,640]{1,0:T(1,128)}, f32[1,640]{1,0:T(1,128)S(1)}, u32[]{:S(2)}, u32[]{:S(2)}) collective-permute-start(f32[1,640]{1,0:T(1,128)} %get-tuple-element.67.refs_0_), channel_id=1, source_target_pairs={{0,1},{1,0},{2,3},{3,2},{4,5},{5,4},{6,7},{7,6},{8,9},{9,8},{10,11... | collective-permute-start | bytes 7688 | tf_op jit(solution)/shard_map/ppermute | solution.py:487
  13.0 10.5 %collective-permute-start.3 = (bf16[2048,128]{1,0:T(8,128)(2,1)S(1)}, bf16[2048,128]{1,0:T(8,128)(2,1)S(1)}, u32[]{:S(2)}, u32[]{:S(2)}) collective-permute-start(bf16[2048,128]{1,0:T(8,128)(2,1)S(1)} %get-tuple-element.70), channel_id=1, source_target_pairs={{0,16},{16,0},{1,17},{17,1},{2,18},{18,2},{3,19},{19,3},{4,20},{20... | collective-permute-start | bytes 1572872 | tf_op jit(solution)/shard_map/ppermute | solution.py:482
  13.6 17.7 %collective-permute-start.8 = (bf16[1280,128]{1,0:T(8,128)(2,1)S(1)}, bf16[1280,128]{1,0:T(8,128)(2,1)S(1)}, u32[]{:S(2)}, u32[]{:S(2)}) collective-permute-start(bf16[1280,128]{1,0:T(8,128)(2,1)S(1)} %get-tuple-element.79), channel_id=1, source_target_pairs={{0,16},{16,0},{1,17},{17,1},{2,18},{18,2},{3,19},{19,3},{4,20},{20... | collective-permute-start | bytes 983048 | tf_op jit(solution)/shard_map/ppermute | solution.py:482
  15.5 17.7 %collective-permute-start.5 = (bf16[640,128]{1,0:T(8,128)(2,1)S(1)}, bf16[640,128]{1,0:T(8,128)(2,1)S(1)}, u32[]{:S(2)}, u32[]{:S(2)}) collective-permute-start(bf16[640,128]{1,0:T(8,128)(2,1)S(1)} %get-tuple-element.75), channel_id=1, source_target_pairs={{0,4},{4,0},{8,12},{12,8},{16,20},{28,24},{1,5},{5,1},{9,13},{13,9... | collective-permute-start | bytes 491528 | tf_op jit(solution)/shard_map/ppermute | solution.py:479
  19.0 19.5 %collective-permute-start.6 = (bf16[640,128]{1,0:T(8,128)(2,1)S(1)}, bf16[640,128]{1,0:T(8,128)(2,1)S(1)}, u32[]{:S(2)}, u32[]{:S(2)}) collective-permute-start(bf16[640,128]{1,0:T(8,128)(2,1)S(1)} %get-tuple-element.76), channel_id=1, source_target_pairs={{0,8},{4,12},{8,0},{12,4},{16,24},{28,20},{1,9},{5,13},{9,1},{13,5... | collective-permute-start | bytes 491528 | tf_op jit(solution)/shard_map/ppermute | solution.py:479
  23.6 35.6 %collective-permute-start.16 = (bf16[1024,128]{1,0:T(8,128)(2,1)S(1)}, bf16[1024,128]{1,0:T(8,128)(2,1)S(1)}, u32[]{:S(2)}, u32[]{:S(2)}) collective-permute-start(bf16[1024,128]{1,0:T(8,128)(2,1)S(1)} %get-tuple-element.93), channel_id=1, source_target_pairs={{0,12},{4,8},{8,4},{12,0},{20,24},{24,20},{1,13},{5,9},{9,5},{13,1... | collective-permute-start | bytes 786440 | tf_op jit(solution)/shard_map/ppermute | solution.py:479
  25.7 17.2 %collective-permute-start.7 = (bf16[640,128]{1,0:T(8,128)(2,1)S(1)}, bf16[640,128]{1,0:T(8,128)(2,1)S(1)}, u32[]{:S(2)}, u32[]{:S(2)}) collective-permute-start(bf16[640,128]{1,0:T(8,128)(2,1)S(1)} %get-tuple-element.77), channel_id=1, source_target_pairs={{0,12},{4,8},{8,4},{12,0},{20,24},{24,20},{1,13},{5,9},{9,5},{13,1... | collective-permute-start | bytes 491528 | tf_op jit(solution)/shard_map/ppermute | solution.py:479
  31.3 11.6 %collective-permute-start.9 = (bf16[640,128]{1,0:T(8,128)(2,1)S(1)}, bf16[640,128]{1,0:T(8,128)(2,1)S(1)}, u32[]{:S(2)}, u32[]{:S(2)}) collective-permute-start(bf16[640,128]{1,0:T(8,128)(2,1)S(1)} %get-tuple-element.81), channel_id=1, source_target_pairs={{0,4},{4,0},{8,12},{12,8},{16,20},{28,24},{1,5},{5,1},{9,13},{13,9... | collective-permute-start | bytes 491528 | tf_op jit(solution)/shard_map/ppermute | solution.py:479
  33.3 18.3 %collective-permute-start.10 = (bf16[640,128]{1,0:T(8,128)(2,1)S(1)}, bf16[640,128]{1,0:T(8,128)(2,1)S(1)}, u32[]{:S(2)}, u32[]{:S(2)}) collective-permute-start(bf16[640,128]{1,0:T(8,128)(2,1)S(1)} %get-tuple-element.82), channel_id=1, source_target_pairs={{0,8},{4,12},{8,0},{12,4},{16,24},{28,20},{1,9},{5,13},{9,1},{13,5... | collective-permute-start | bytes 491528 | tf_op jit(solution)/shard_map/ppermute | solution.py:479
  38.5 13.1 %collective-permute-start.11 = (bf16[640,128]{1,0:T(8,128)(2,1)S(1)}, bf16[640,128]{1,0:T(8,128)(2,1)S(1)}, u32[]{:S(2)}, u32[]{:S(2)}) collective-permute-start(bf16[640,128]{1,0:T(8,128)(2,1)S(1)} %get-tuple-element.83), channel_id=1, source_target_pairs={{0,12},{4,8},{8,4},{12,0},{20,24},{24,20},{1,13},{5,9},{9,5},{13,1... | collective-permute-start | bytes 491528 | tf_op jit(solution)/shard_map/ppermute | solution.py:479
  52.0 26.4 %collective-permute-start.12 = (bf16[1024,128]{1,0:T(8,128)(2,1)S(1)}, bf16[1024,128]{1,0:T(8,128)(2,1)S(1)}, u32[]{:S(2)}, u32[]{:S(2)}) collective-permute-start(bf16[1024,128]{1,0:T(8,128)(2,1)S(1)} %get-tuple-element.89), channel_id=1, source_target_pairs={{0,4},{4,0},{8,12},{12,8},{16,20},{28,24},{1,5},{5,1},{9,13},{13,9... | collective-permute-start | bytes 786440 | tf_op jit(solution)/shard_map/ppermute | solution.py:479
  56.3 14.8 %collective-permute-start.14 = (bf16[1024,128]{1,0:T(8,128)(2,1)S(1)}, bf16[1024,128]{1,0:T(8,128)(2,1)S(1)}, u32[]{:S(2)}, u32[]{:S(2)}) collective-permute-start(bf16[1024,128]{1,0:T(8,128)(2,1)S(1)} %get-tuple-element.91), channel_id=1, source_target_pairs={{0,8},{4,12},{8,0},{12,4},{16,24},{28,20},{1,9},{5,13},{9,1},{13,5... | collective-permute-start | bytes 786440 | tf_op jit(solution)/shard_map/ppermute | solution.py:479
  64.6 36.4 %collective-permute-start.17 = (bf16[1024,128]{1,0:T(8,128)(2,1)S(1)}, bf16[1024,128]{1,0:T(8,128)(2,1)S(1)}, u32[]{:S(2)}, u32[]{:S(2)}) collective-permute-start(bf16[1024,128]{1,0:T(8,128)(2,1)S(1)} %get-tuple-element.94), channel_id=1, source_target_pairs={{0,12},{4,8},{8,4},{12,0},{20,24},{24,20},{1,13},{5,9},{9,5},{13,1... | collective-permute-start | bytes 786440 | tf_op jit(solution)/shard_map/ppermute | solution.py:479
  76.5 26.1 %collective-permute-start.15 = (bf16[1024,128]{1,0:T(8,128)(2,1)S(1)}, bf16[1024,128]{1,0:T(8,128)(2,1)S(1)}, u32[]{:S(2)}, u32[]{:S(2)}) collective-permute-start(bf16[1024,128]{1,0:T(8,128)(2,1)S(1)} %get-tuple-element.92), channel_id=1, source_target_pairs={{0,8},{4,12},{8,0},{12,4},{20,28},{24,16},{1,9},{5,13},{9,1},{13,5... | collective-permute-start | bytes 786440 | tf_op jit(solution)/shard_map/ppermute | solution.py:479
  83.9 19.2 %collective-permute-start.13 = (bf16[1024,128]{1,0:T(8,128)(2,1)S(1)}, bf16[1024,128]{1,0:T(8,128)(2,1)S(1)}, u32[]{:S(2)}, u32[]{:S(2)}) collective-permute-start(bf16[1024,128]{1,0:T(8,128)(2,1)S(1)} %get-tuple-element.90), channel_id=1, source_target_pairs={{0,4},{4,0},{8,12},{12,8},{20,16},{24,28},{1,5},{5,1},{9,13},{13,9... | collective-permute-start | bytes 786440 | tf_op jit(solution)/shard_map/ppermute | solution.py:479
  94.8 17.4 %collective-permute-start.29 = (bf16[672,128]{1,0:T(8,128)(2,1)S(1)}, bf16[672,128]{1,0:T(8,128)(2,1)S(1)}, u32[]{:S(2)}, u32[]{:S(2)}) collective-permute-start(bf16[672,128]{1,0:T(8,128)(2,1)S(1)} %get-tuple-element.118), channel_id=1, source_target_pairs={{0,4},{4,0},{8,12},{12,8},{20,16},{24,28},{1,5},{5,1},{9,13},{13,9... | collective-permute-start | bytes 516104 | tf_op jit(solution)/shard_map/ppermute | solution.py:479
  96.7 19.8 %collective-permute-start.30 = (bf16[672,128]{1,0:T(8,128)(2,1)S(1)}, bf16[672,128]{1,0:T(8,128)(2,1)S(1)}, u32[]{:S(2)}, u32[]{:S(2)}) collective-permute-start(bf16[672,128]{1,0:T(8,128)(2,1)S(1)} %get-tuple-element.119), channel_id=1, source_target_pairs={{0,8},{4,12},{8,0},{12,4},{20,28},{24,16},{1,9},{5,13},{9,1},{13,5... | collective-permute-start | bytes 516104 | tf_op jit(solution)/shard_map/ppermute | solution.py:479
  101.1 4.6 %collective-permute-start.24 = (f32[1,2560]{1,0:T(1,128)S(1)}, f32[1,2560]{1,0:T(1,128)S(1)}, u32[]{:S(2)}, u32[]{:S(2)}) collective-permute-start(f32[1,2560]{1,0:T(1,128)S(1)} %get-tuple-element.111.refs_0_), channel_id=1, source_target_pairs={{0,3},{1,2},{2,1},{3,0},{4,7},{5,6},{6,5},{7,4},{8,11},{9,10},{10,... | collective-permute-start | bytes 30728 | tf_op jit(solution)/shard_map/ppermute | solution.py:487
  102.7 3.7 %collective-permute-start.23 = (f32[1,2560]{1,0:T(1,128)S(1)}, f32[1,2560]{1,0:T(1,128)S(1)}, u32[]{:S(2)}, u32[]{:S(2)}) collective-permute-start(f32[1,2560]{1,0:T(1,128)S(1)} %get-tuple-element.111.refs_0_), channel_id=1, source_target_pairs={{0,2},{1,3},{2,0},{3,1},{4,6},{5,7},{6,4},{7,5},{8,10},{9,11},{10,... | collective-permute-start | bytes 30728 | tf_op jit(solution)/shard_map/ppermute | solution.py:487
  103.2 7.0 %collective-permute-start.22 = (f32[1,2560]{1,0:T(1,128)S(1)}, f32[1,2560]{1,0:T(1,128)S(1)}, u32[]{:S(2)}, u32[]{:S(2)}) collective-permute-start(f32[1,2560]{1,0:T(1,128)S(1)} %get-tuple-element.111.refs_0_), channel_id=1, source_target_pairs={{0,1},{1,0},{2,3},{3,2},{4,5},{5,4},{6,7},{7,6},{8,9},{9,8},{10,11... | collective-permute-start | bytes 30728 | tf_op jit(solution)/shard_map/ppermute | solution.py:487
  105.7 20.2 %collective-permute-start.18 = (bf16[2048,128]{1,0:T(8,128)(2,1)S(1)}, bf16[2048,128]{1,0:T(8,128)(2,1)S(1)}, u32[]{:S(2)}, u32[]{:S(2)}) collective-permute-start(bf16[2048,128]{1,0:T(8,128)(2,1)S(1)} %shard_map.172), channel_id=1, source_target_pairs={{0,16},{16,0},{1,17},{17,1},{2,18},{18,2},{3,19},{19,3},{4,20},{20... | collective-permute-start | bytes 1572872 | tf_op jit(solution)/shard_map/ppermute | solution.py:482
  106.3 14.1 %collective-permute-start.31 = (bf16[672,128]{1,0:T(8,128)(2,1)S(1)}, bf16[672,128]{1,0:T(8,128)(2,1)S(1)}, u32[]{:S(2)}, u32[]{:S(2)}) collective-permute-start(bf16[672,128]{1,0:T(8,128)(2,1)S(1)} %get-tuple-element.120), channel_id=1, source_target_pairs={{0,12},{4,8},{8,4},{12,0},{20,24},{24,20},{1,13},{5,9},{9,5},{13,1... | collective-permute-start | bytes 516104 | tf_op jit(solution)/shard_map/ppermute | solution.py:479
  110.3 10.3 %collective-permute-start.25 = (bf16[672,128]{1,0:T(8,128)(2,1)S(1)}, bf16[672,128]{1,0:T(8,128)(2,1)S(1)}, u32[]{:S(2)}, u32[]{:S(2)}) collective-permute-start(bf16[672,128]{1,0:T(8,128)(2,1)S(1)} %get-tuple-element.113), channel_id=1, source_target_pairs={{0,4},{4,0},{8,12},{12,8},{20,16},{24,28},{1,5},{5,1},{9,13},{13,9... | collective-permute-start | bytes 516104 | tf_op jit(solution)/shard_map/ppermute | solution.py:479
  112.2 10.9 %collective-permute-start.26 = (bf16[672,128]{1,0:T(8,128)(2,1)S(1)}, bf16[672,128]{1,0:T(8,128)(2,1)S(1)}, u32[]{:S(2)}, u32[]{:S(2)}) collective-permute-start(bf16[672,128]{1,0:T(8,128)(2,1)S(1)} %get-tuple-element.114), channel_id=1, source_target_pairs={{0,8},{4,12},{8,0},{12,4},{20,28},{24,16},{1,9},{5,13},{9,1},{13,5... | collective-permute-start | bytes 516104 | tf_op jit(solution)/shard_map/ppermute | solution.py:479
  116.6 9.2 %collective-permute-start.27 = (bf16[672,128]{1,0:T(8,128)(2,1)S(1)}, bf16[672,128]{1,0:T(8,128)(2,1)S(1)}, u32[]{:S(2)}, u32[]{:S(2)}) collective-permute-start(bf16[672,128]{1,0:T(8,128)(2,1)S(1)} %get-tuple-element.115), channel_id=1, source_target_pairs={{0,12},{4,8},{8,4},{12,0},{20,24},{24,20},{1,13},{5,9},{9,5},{13,1... | collective-permute-start | bytes 516104 | tf_op jit(solution)/shard_map/ppermute | solution.py:479
  120.5 10.0 %collective-permute-start.32 = (bf16[1344,128]{1,0:T(8,128)(2,1)S(1)}, bf16[1344,128]{1,0:T(8,128)(2,1)S(1)}, u32[]{:S(2)}, u32[]{:S(2)}) collective-permute-start(bf16[1344,128]{1,0:T(8,128)(2,1)S(1)} %shard_map.179), channel_id=1, source_target_pairs={{0,16},{16,0},{1,17},{17,1},{2,18},{18,2},{3,19},{19,3},{4,20},{20... | collective-permute-start | bytes 1032200 | tf_op jit(solution)/shard_map/ppermute | solution.py:482
  125.8 6.9 %collective-permute-start.28 = (bf16[1344,128]{1,0:T(8,128)(2,1)S(1)}, bf16[1344,128]{1,0:T(8,128)(2,1)S(1)}, u32[]{:S(2)}, u32[]{:S(2)}) collective-permute-start(bf16[1344,128]{1,0:T(8,128)(2,1)S(1)} %shard_map.177), channel_id=1, source_target_pairs={{0,16},{16,0},{1,17},{17,1},{2,18},{18,2},{3,19},{19,3},{4,20},{20... | collective-permute-start | bytes 1032200 | tf_op jit(solution)/shard_map/ppermute | solution.py:482
  127.0 7.0 %collective-permute-start.21 = (f32[1,256]{1,0:T(1,128)S(1)}, f32[1,256]{1,0:T(1,128)S(1)}, u32[]{:S(2)}, u32[]{:S(2)}) collective-permute-start(f32[1,256]{1,0:T(1,128)S(1)} %get-tuple-element.96.refs_0_), channel_id=1, source_target_pairs={{0,3},{1,2},{2,1},{3,0},{4,7},{5,6},{6,5},{7,4},{8,11},{9,10},{10,... | collective-permute-start | bytes 3080 | tf_op jit(solution)/shard_map/ppermute | solution.py:487
  128.4 5.5 %collective-permute-start.20 = (f32[1,256]{1,0:T(1,128)S(1)}, f32[1,256]{1,0:T(1,128)S(1)}, u32[]{:S(2)}, u32[]{:S(2)}) collective-permute-start(f32[1,256]{1,0:T(1,128)S(1)} %get-tuple-element.96.refs_0_), channel_id=1, source_target_pairs={{0,2},{1,3},{2,0},{3,1},{4,6},{5,7},{6,4},{7,5},{8,10},{9,11},{10,... | collective-permute-start | bytes 3080 | tf_op jit(solution)/shard_map/ppermute | solution.py:487
  129.9 4.0 %collective-permute-start.19 = (f32[1,256]{1,0:T(1,128)S(1)}, f32[1,256]{1,0:T(1,128)S(1)}, u32[]{:S(2)}, u32[]{:S(2)}) collective-permute-start(f32[1,256]{1,0:T(1,128)S(1)} %get-tuple-element.96.refs_0_), channel_id=1, source_target_pairs={{0,1},{1,0},{2,3},{3,2},{4,5},{5,4},{6,7},{7,6},{8,9},{9,8},{10,11... | collective-permute-start | bytes 3080 | tf_op jit(solution)/shard_map/ppermute | solution.py:487
  (9 other events, 75.6 us)
